TPU v7x, 768 devices: a whole 4x8x12 slice. The times are simulated.
768 devices in a mesh: energy: 32 (over y, x_lo, core), space: 24 (over z, x_hi).
Axes of the slice: x: 4 (x_hi: 2, x_lo: 2; x = x_hi * 2 + x_lo), y: 8, z: 12, core: 2. Of those that a mesh axis runs over, the one named last changes fastest.
Arguments:
- greens: bfloat16 [2, 2, 32, 3072, 128], P(None, None, 'energy', 'space'), may hold values from -6 to 6
- coulomb: bfloat16 [3, 3072, 128], P(None, 'space'), may hold values from -0.3125 to 0.3125
- pattern: int32 [24, 2], P('space'), may hold values 0 or 1
Outputs:
- polar_sides: bfloat16 [2, 2, 2, 32, 3072, 128], P(None, None, None, 'energy', 'space')
- screened: bfloat16 [2, 2, 32, 3072, 128], P(None, None, 'energy', 'space')
Inputs may be any that keep to these rules, and one draw needn't show every extreme that they name: pattern holds only 0 and 1.
All inputs are finite; a program needn't handle non-finite values. No bound on the sum of `pattern` on one device may be relied on, other than what follows from the above.
Results may differ from a plain program's by a relative error of at most 0.0077.
Values may be sent and summed in bfloat16 or wider, within the bound.
A program may use at most 32 MiB of HBM per device.

v0:
```python
import math

import jax
import jax.numpy as jnp
from jax import lax
from jax.sharding import PartitionSpec as P


def extended(cells, sides, width):
    for axis, dim in sides:
        count = lax.axis_size(axis)
        ends = count - 1
        head = lax.slice_in_dim(cells, 0, width, axis=dim)
        tail = lax.slice_in_dim(cells, cells.shape[dim] - width, cells.shape[dim], axis=dim)
        cells = jnp.concatenate(
            [
                lax.ppermute(tail, axis, [(i, (i + 1) % count) for i in range(ends)]),
                cells,
                lax.ppermute(head, axis, [((i + 1) % count, i) for i in range(ends)]),
            ],
            axis=dim,
        )
    return cells


def make_tables(energies):
    period = 2 * energies
    times = jnp.arange(period, dtype=jnp.int32)
    levels = jnp.arange(energies, dtype=jnp.int32)
    phases = (times[:, None] * levels[None, :] % period).astype(jnp.float32) * jnp.float32(
        2.0 * math.pi / period
    )
    cos_part = jnp.cos(phases)
    sin_part = jnp.sin(phases)
    forward_table = jnp.concatenate(
        [
            jnp.concatenate([cos_part, sin_part], axis=1),
            jnp.concatenate([-sin_part, cos_part], axis=1),
        ],
        axis=0,
    ).astype(jnp.bfloat16)
    cos_back = cos_part.T
    sin_back = sin_part.T
    factor = 1.0 / (period * math.sqrt(energies))
    rows_list = [
        jnp.concatenate([cos_back, -sin_back], axis=1),
        jnp.concatenate([sin_back, cos_back], axis=1),
        jnp.concatenate([-cos_back, -sin_back], axis=1),
        jnp.concatenate([-sin_back, cos_back], axis=1),
    ]
    inverse_table = (jnp.concatenate(rows_list, axis=0) * jnp.float32(factor)).astype(jnp.bfloat16)
    return (forward_table, inverse_table)


def time_product(time_fields, period):
    less_re = time_fields[0, :period]
    less_im = time_fields[0, period:]
    great_re = time_fields[1, :period]
    great_im = time_fields[1, period:]
    real_part = less_re * great_im - less_im * great_re
    imag_part = less_re * great_re + less_im * great_im
    return jnp.concatenate([real_part, imag_part], axis=0).astype(jnp.bfloat16)


def project(coupling, blocks):
    shape_kept = blocks.shape
    flat_blocks = blocks.reshape(-1, shape_kept[-2], shape_kept[-1])
    result = jnp.matmul(coupling[None], flat_blocks, preferred_element_type=jnp.float32)
    return result.astype(jnp.bfloat16).reshape(shape_kept)


def closing(image, coupling):
    shape_kept = image.shape
    flat_rows = image.reshape(-1, shape_kept[-1])
    result = jnp.dot(flat_rows, coupling.T, preferred_element_type=jnp.float32)
    return result.reshape(shape_kept[:-1] + (coupling.shape[0],))


def local(greens, coulomb, pattern):
    e_dev = greens.shape[2]
    block_size = greens.shape[-1]
    energies = e_dev * lax.axis_size("energy")
    period = 2 * energies
    forward_table, inverse_table = make_tables(energies)
    flat_rows = greens.reshape(2, 2, e_dev, block_size * block_size)
    regrouped = lax.all_to_all(flat_rows, "energy", split_axis=3, concat_axis=2, tiled=True)
    elements = regrouped.shape[3]
    stacked = regrouped.reshape(2, 2 * energies, elements)
    time_fields = jnp.einsum(
        "tk,akn->atn", forward_table, stacked, preferred_element_type=jnp.float32
    )
    product = time_product(time_fields, period)
    spectra = jnp.dot(inverse_table, product, preferred_element_type=jnp.float32).astype(
        jnp.bfloat16
    )
    spectra = spectra.reshape(2, 2, energies, elements)
    link_marks = pattern.astype(jnp.bfloat16)
    lower_coupling = coulomb[0] * link_marks[0, 0]
    diag_coupling = coulomb[1]
    upper_coupling = coulomb[2] * link_marks[0, 1]
    returned = lax.all_to_all(spectra, "energy", split_axis=2, concat_axis=3, tiled=True)
    item_count = returned.shape[0]
    blocks = returned.reshape(item_count, 2, e_dev, block_size, block_size)
    padded = extended(blocks, (("space", 3),), block_size)
    below_block = padded[:, :, :, :block_size]
    above_block = padded[:, :, :, 2 * block_size :]
    side_lower = project(lower_coupling, below_block)
    side_upper = project(upper_coupling, above_block)
    own_image = project(diag_coupling, blocks)
    summed = (
        closing(side_lower, lower_coupling)
        + closing(own_image, diag_coupling)
        + closing(side_upper, upper_coupling)
    )
    polar_sides = jnp.stack([side_lower, side_upper], axis=1)
    screened = summed.astype(jnp.bfloat16)
    return (polar_sides, screened)


def solution(mesh):
    placed = (P(None, None, "energy", "space", None), P(None, "space", None), P("space", None))
    return jax.shard_map(
        local,
        mesh=mesh,
        in_specs=placed,
        out_specs=(
            P(None, None, None, "energy", "space", None),
            P(None, None, "energy", "space", None),
        ),
        check_vma=False,
    )
```

profile of v0, /device:TPU:512, one launch (start us, length us, event | category | flops | bytes accessed | tf_op | source)
XLA Modules:
  0.0 115.3 jit_solution(16209997873535614485)
XLA Ops:
  0.6 10.9 %copy.23 = bf16[2,2,1,128,128]{1,0,4,3,2:T(2,128)(2,1)} copy(bf16[2,2,1,128,128]{4,3,2,1,0:T(8,128)(2,1)} %param.3) | data formatting | bytes 262144 | tf_op args[0]
  11.6 13.7 %reshape.72 = bf16[32,2,1024]{2,1,0:T(2,128)(2,1)} reshape(bf16[16384,1,2,2]{3,2,1,0:T(2,128)(2,1)} %bitcast.82) | data formatting | bytes 262144
  25.3 8.4 %all-to-all-start = ((bf16[32,2,1024]{2,1,0:T(2,128)(2,1)}), bf16[32,2,1024]{2,1,0:T(2,128)(2,1)S(1)}, u32[]{:S(2)}, u32[]{:S(2)}) async-start(bf16[32,2,1024]{2,1,0:T(2,128)(2,1)} %reshape.72), calls=%async_computation | async-start | bytes 262144 | tf_op jit(solution)/shard_map/all_to_all | solution.py:86
  33.7 0.1 negate_convert_fusion
  34.0 0.1 fusion.45
  34.1 9.2 %all-to-all-done = bf16[32,2,1024]{2,1,0:T(2,128)(2,1)S(1)} async-done(((bf16[32,2,1024]{2,1,0:T(2,128)(2,1)}), bf16[32,2,1024]{2,1,0:T(2,128)(2,1)S(1)}, u32[]{:S(2)}, u32[]{:S(2)}) %all-to-all-start) | async-done | bytes 131104 | tf_op jit(solution)/shard_map/all_to_all | solution.py:86
  43.3 19.1 %reshape.73 = bf16[16384,1,2,2]{3,2,1,0:T(2,128)(2,1)} reshape(bf16[32,2,1024]{2,1,0:T(2,128)(2,1)S(1)} %all-to-all-done) | data formatting | bytes 262144
  62.4 16.4 %copy.24 = bf16[2,2,1,16384]{3,1,0,2:T(2,128)(2,1)S(1)} copy(bf16[2,2,1,16384]{1,0,2,3:T(2,128)(2,1)} %bitcast.81) | data formatting | bytes 262144 | tf_op jit(solution)/shard_map/all_to_all | solution.py:86
  78.9 0.3 convolution_bitcast_fusion
  79.3 0.2 convolution_convert_fusion.3
  79.5 0.8 copy.25
  80.3 3.9 %all-to-all-start.1 = ((bf16[2,2,32,512]{3,1,0,2:T(2,128)(2,1)}), bf16[2,2,32,512]{3,1,0,2:T(2,128)(2,1)S(1)}, u32[]{:S(2)}, u32[]{:S(2)}) async-start(bf16[2,2,32,512]{3,1,0,2:T(2,128)(2,1)} %copy.25), calls=%async_computation.1 | async-start | bytes 262144 | tf_op jit(solution)/shard_map/all_to_all | solution.py:101
  84.2 0.6 fusion.51
  84.8 8.9 %all-to-all-done.1 = bf16[2,2,32,512]{3,1,0,2:T(2,128)(2,1)S(1)} async-done(((bf16[2,2,32,512]{3,1,0,2:T(2,128)(2,1)}), bf16[2,2,32,512]{3,1,0,2:T(2,128)(2,1)S(1)}, u32[]{:S(2)}, u32[]{:S(2)}) %all-to-all-start.1) | async-done | bytes 131104 | tf_op jit(solution)/shard_map/all_to_all | solution.py:101
  93.9 5.8 %collective-permute-start.1 = (bf16[2,2,1,128,128]{4,3,1,0,2:T(8,128)(2,1)S(1)}, bf16[2,2,1,128,128]{4,3,1,0,2:T(8,128)(2,1)S(1)}, u32[]{:S(2)}, u32[]{:S(2)}) collective-permute-start(bf16[2,2,1,128,128]{4,3,1,0,2:T(8,128)(2,1)S(1)} %reshape.62), channel_id=1, source_target_pairs={{1,0},{2,1},{3,2},{4,3},{5,4},{6,5},{7,6},{8,7},{9,8},{10,9},{11,1... | collective-permute-start | bytes 393224 | tf_op jit(solution)/shard_map/ppermute | solution.py:19
  99.7 1.9 %collective-permute-start = (bf16[2,2,1,128,128]{4,3,1,0,2:T(8,128)(2,1)S(1)}, bf16[2,2,1,128,128]{4,3,1,0,2:T(8,128)(2,1)S(1)}, u32[]{:S(2)}, u32[]{:S(2)}) collective-permute-start(bf16[2,2,1,128,128]{4,3,1,0,2:T(8,128)(2,1)S(1)} %reshape.62), channel_id=1, source_target_pairs={{0,1},{1,2},{2,3},{3,4},{4,5},{5,6},{6,7},{7,8},{8,9},{9,10},{10,1... | collective-permute-start | bytes 393224 | tf_op jit(solution)/shard_map/ppermute | solution.py:17
  101.8 0.2 convolution_convert_fusion
  102.0 8.4 %collective-permute-done = bf16[2,2,1,128,128]{4,3,1,0,2:T(8,128)(2,1)S(1)} collective-permute-done((bf16[2,2,1,128,128]{4,3,1,0,2:T(8,128)(2,1)S(1)}, bf16[2,2,1,128,128]{4,3,1,0,2:T(8,128)(2,1)S(1)}, u32[]{:S(2)}, u32[]{:S(2)}) %collective-permute-start) | collective-permute-done | bytes 131104 | tf_op jit(solution)/shard_map/ppermute | solution.py:17
  110.4 0.8 convolution_convert_fusion.2
  111.3 0.8 fusion.11
  112.1 0.8 convolution_convert_fusion.1
  112.9 0.7 pad_maximum_fusion
  113.6 0.2 convolution_add_fusion.1
  113.9 1.5 %fusion.1 = bf16[2,2,1,128,128]{4,3,2,1,0:T(8,128)(2,1)} fusion(f32[2,2,128,128]{3,2,1,0:T(8,128)S(1)} %convolution_add_fusion.1, bf16[2,2,128,128]{3,2,1,0:T(8,128)(2,1)S(1)} %bitcast.84, bf16[3,128,128]{2,1,0:T(8,128)(2,1)S(1)} %copy-done, bf16[]{:T(256)} %bitcast.13), kind=kOutput, calls=%fused_computation.8 | convolution fusion | flops 16924672 | bytes 557058 | tf_op jit(solution)/shard_map/dot_general | solution.py:75
  (13 shorter events, 0.5 us)
Async XLA Ops:
  25.3 18.0 %all-to-all-start = ((bf16[32,2,1024]{2,1,0:T(2,128)(2,1)}), bf16[32,2,1024]{2,1,0:T(2,128)(2,1)S(1)}, u32[]{:S(2)}, u32[]{:S(2)}) async-start(bf16[32,2,1024]{2,1,0:T(2,128)(2,1)} %reshape.72), calls=%async_computation | async-start | bytes 262144 | tf_op jit(solution)/shard_map/all_to_all | solution.py:86
  34.1 50.1 %copy-start.1 = (s32[1,2]{1,0:T(1,128)S(1)}, s32[1,2]{1,0:T(1,128)}, u32[]{:S(2)}) copy-start(s32[1,2]{1,0:T(1,128)} %param.5) | copy-start | bytes 28
  34.1 67.7 %copy-start = (bf16[3,128,128]{2,1,0:T(8,128)(2,1)S(1)}, bf16[3,128,128]{2,1,0:T(8,128)(2,1)}, u32[]{:S(2)}) copy-start(bf16[3,128,128]{2,1,0:T(8,128)(2,1)} %param.4) | copy-start | bytes 294916
  80.3 13.4 %all-to-all-start.1 = ((bf16[2,2,32,512]{3,1,0,2:T(2,128)(2,1)}), bf16[2,2,32,512]{3,1,0,2:T(2,128)(2,1)S(1)}, u32[]{:S(2)}, u32[]{:S(2)}) async-start(bf16[2,2,32,512]{3,1,0,2:T(2,128)(2,1)} %copy.25), calls=%async_computation.1 | async-start | bytes 262144 | tf_op jit(solution)/shard_map/all_to_all | solution.py:101
  93.9 18.2 %collective-permute-start.1 = (bf16[2,2,1,128,128]{4,3,1,0,2:T(8,128)(2,1)S(1)}, bf16[2,2,1,128,128]{4,3,1,0,2:T(8,128)(2,1)S(1)}, u32[]{:S(2)}, u32[]{:S(2)}) collective-permute-start(bf16[2,2,1,128,128]{4,3,1,0,2:T(8,128)(2,1)S(1)} %reshape.62), channel_id=1, source_target_pairs={{1,0},{2,1},{3,2},{4,3},{5,4},{6,5},{7,6},{8,7},{9,8},{10,9},{11,1... | collective-permute-start | bytes 393224 | tf_op jit(solution)/shard_map/ppermute | solution.py:19
  99.7 10.7 %collective-permute-start = (bf16[2,2,1,128,128]{4,3,1,0,2:T(8,128)(2,1)S(1)}, bf16[2,2,1,128,128]{4,3,1,0,2:T(8,128)(2,1)S(1)}, u32[]{:S(2)}, u32[]{:S(2)}) collective-permute-start(bf16[2,2,1,128,128]{4,3,1,0,2:T(8,128)(2,1)S(1)} %reshape.62), channel_id=1, source_target_pairs={{0,1},{1,2},{2,3},{3,4},{4,5},{5,6},{6,7},{7,8},{8,9},{9,10},{10,1... | collective-permute-start | bytes 393224 | tf_op jit(solution)/shard_map/ppermute | solution.py:17
where the time goes:
time: 117 us; the launch traced here: 115 us
  local copies, waits for them, and re-layouts  61.9 us (53%)
  waiting for transfers between devices  26.6 us (23%)
  starting transfers between devices  20 us (17%)
  matrix products  4.9 us (4%)
    unnamed x7, local copies, waits for them, and re-layouts  43.8 us
    all_to_all x1, local copies, waits for them, and re-layouts, local(): lax.all_to_all(flat_rows, 'energy', split_axis=3, concat_axis=2, tiled=True)  16.4 us
    all_to_all x1, waiting for transfers between devices, local(): lax.all_to_all(flat_rows, 'energy', split_axis=3, concat_axis=2, tiled=True)  9.22 us
    all_to_all x1, waiting for transfers between devices, local(): lax.all_to_all(spectra, 'energy', split_axis=2, concat_axis=3, tiled=True)  8.94 us
    ppermute x1, waiting for transfers between devices, extended(): lax.ppermute(tail, axis, [(i, (i + 1) % count) for i in range(ends)])  8.43 us
    all_to_all x1, starting transfers between devices, local(): lax.all_to_all(flat_rows, 'energy', split_axis=3, concat_axis=2, tiled=True)  8.42 us
    ppermute x1, starting transfers between devices, extended(): lax.ppermute(head, axis, [((i + 1) % count, i) for i in range(ends)])  5.84 us
    all_to_all x1, starting transfers between devices, local(): lax.all_to_all(spectra, 'energy', split_axis=2, concat_axis=3, tiled=True)  3.86 us
  transfers between devices with their start and end apart: 4, of which 3 were waited for; matrix products, arithmetic and copies ran while one was open for 3% of the time, Pallas kernels for 0%

commit v1 on v0

v1 whole, which is shorter than its diff:
```python
import math

import jax
import jax.numpy as jnp
import numpy as np
from jax import lax
from jax.experimental import pallas as pl
from jax.experimental.pallas import tpu as pltpu
from jax.sharding import PartitionSpec as P

MESH = pl.DeviceIdType.MESH
BF16 = jnp.bfloat16


def make_tables(energies, rows):
    period = 2 * energies
    phases = (np.arange(period)[:, None] * np.arange(energies)[None, :] % period) * (2.0 * math.pi / period)
    cos_part, sin_part = np.cos(phases), np.sin(phases)
    forward = np.block([[cos_part, sin_part], [-sin_part, cos_part]])
    cos_back, sin_back = cos_part.T, sin_part.T
    inverse = np.block(
        [[cos_back, -sin_back], [sin_back, cos_back], [-cos_back, -sin_back], [-sin_back, cos_back]]
    ) * (1.0 / (period * math.sqrt(energies)))
    unit = np.eye(rows)
    return tuple(np.kron(table, unit).astype(np.float32).astype(BF16) for table in (forward, inverse))


def kernel(
    n_energy, n_space,
    greens, coulomb, pattern, forward, inverse,
    sides, screened,
    own, gathered, spectra, polar, fwd, inv, coul,
    send_sem, gather_sem, return_sem, side_send, side_sem, local_sem,
):
    e = lax.axis_index("energy")
    s = lax.axis_index("space")
    size = own.shape[1]
    rows = size // n_energy
    above = lax.rem(s + 1, n_space)
    below = lax.rem(s + n_space - 1, n_space)

    def peer(k):
        return lax.rem(e + k, n_energy)

    def part(ref, index):
        return ref.at[:, pl.ds(pl.multiple_of(index * rows, rows), rows), :]

    loads = [
        pltpu.make_async_copy(greens, own, local_sem.at[0]),
        pltpu.make_async_copy(forward, fwd, local_sem.at[1]),
        pltpu.make_async_copy(inverse, inv, local_sem.at[2]),
        pltpu.make_async_copy(coulomb, coul, local_sem.at[3]),
    ]
    for load in loads:
        load.start()

    barrier = pltpu.get_barrier_semaphore()

    def greet(k, carry):
        pl.semaphore_signal(barrier, inc=1, device_id={"energy": peer(k)}, device_id_type=MESH)
        return carry

    lax.fori_loop(1, n_energy, greet, 0)
    for other in (above, below):
        pl.semaphore_signal(barrier, inc=1, device_id={"space": other}, device_id_type=MESH)
    pl.semaphore_wait(barrier, n_energy + 1)
    loads[0].wait()

    def exchange(source, target, send, recv):
        def step(k, carry):
            to = peer(k)
            pltpu.make_async_remote_copy(
                src_ref=part(source, to),
                dst_ref=part(target, e),
                send_sem=send,
                recv_sem=recv,
                device_id={"energy": to},
                device_id_type=MESH,
            ).start()
            return carry

        lax.fori_loop(1, n_energy, step, 0)
        mine = pltpu.make_async_copy(part(source, e), part(target, e), local_sem.at[0])
        mine.start()
        mine.wait()

    def settle(ref, sem):
        whole = ref.at[:, pl.ds(0, size - rows), :]
        pltpu.make_async_copy(whole, whole, sem).wait()

    exchange(own, gathered, send_sem.at[0], gather_sem)
    loads[1].wait()
    loads[2].wait()
    settle(gathered, gather_sem)

    half = 2 * size
    stacked = jnp.concatenate(
        [gathered[0:2].reshape(half, size), gathered[2:4].reshape(half, size)], axis=1
    )
    fields = jnp.dot(fwd[...], stacked, preferred_element_type=jnp.float32)
    less_re, less_im = fields[:half, :size], fields[half:, :size]
    great_re, great_im = fields[:half, size:], fields[half:, size:]
    product = jnp.concatenate(
        [less_re * great_im - less_im * great_re, less_re * great_re + less_im * great_im], axis=0
    ).astype(BF16)
    spectra[...] = (
        jnp.dot(inv[...], product, preferred_element_type=jnp.float32).astype(BF16).reshape(4, size, size)
    )

    exchange(spectra, polar.at[0], send_sem.at[1], return_sem)
    settle(polar.at[0], return_sem)

    hops = []
    for slot, other in ((1, above), (2, below)):
        hop = pltpu.make_async_remote_copy(
            src_ref=polar.at[0],
            dst_ref=polar.at[slot],
            send_sem=side_send.at[slot - 1],
            recv_sem=side_sem.at[slot - 1],
            device_id={"space": other},
            device_id_type=MESH,
        )
        hop.start()
        hops.append(hop)

    loads[3].wait()
    has_below = jnp.where(s > 0, pattern[0, 0], 0).astype(jnp.float32)
    has_above = jnp.where(s < n_space - 1, pattern[0, 1], 0).astype(jnp.float32)
    lower = (coul[0].astype(jnp.float32) * has_below).astype(BF16)
    upper = (coul[2].astype(jnp.float32) * has_above).astype(BF16)
    couplings = (coul[1], lower, upper)

    def images(slot):
        wide = jnp.concatenate([polar[slot, i] for i in range(4)], axis=1)
        return jnp.dot(couplings[slot], wide, preferred_element_type=jnp.float32).astype(BF16)

    own_image = images(0)
    for hop in hops:
        hop.wait_recv()
    side_lower = images(1)
    side_upper = images(2)
    weights = jnp.concatenate([lower, coul[1], upper], axis=1)
    for kind in range(2):
        for portion in range(2):
            i = 2 * kind + portion
            cut = slice(i * size, (i + 1) * size)
            sides[kind, 0, portion, 0] = side_lower[:, cut]
            sides[kind, 1, portion, 0] = side_upper[:, cut]
            joined = jnp.concatenate([side_lower[:, cut], own_image[:, cut], side_upper[:, cut]], axis=1)
            screened[kind, portion, 0] = lax.dot_general(
                joined, weights, (((1,), (1,)), ((), ())), preferred_element_type=jnp.float32
            ).astype(BF16)

    settle(own, send_sem.at[0])
    settle(spectra, send_sem.at[1])
    for hop in hops:
        hop.wait_send()


def solution(mesh):
    n_energy, n_space = mesh.shape["energy"], mesh.shape["space"]

    def local(greens, coulomb, pattern):
        size = greens.shape[-1]
        rows = size // n_energy
        forward, inverse = make_tables(n_energy, rows)
        blocks = pltpu.VMEM((4, size, size), BF16)
        anywhere = pl.BlockSpec(memory_space=pl.ANY)
        vmem = pl.BlockSpec(memory_space=pltpu.VMEM)
        return pl.pallas_call(
            lambda *refs: kernel(n_energy, n_space, *refs),
            out_shape=(
                jax.ShapeDtypeStruct((2, 2, 2, 1, size, size), BF16),
                jax.ShapeDtypeStruct((2, 2, 1, size, size), BF16),
            ),
            in_specs=[anywhere, anywhere, pl.BlockSpec(memory_space=pltpu.SMEM), anywhere, anywhere],
            out_specs=(vmem, vmem),
            scratch_shapes=[
                blocks, blocks, blocks,
                pltpu.VMEM((3, 4, size, size), BF16),
                pltpu.VMEM(forward.shape, BF16),
                pltpu.VMEM(inverse.shape, BF16),
                pltpu.VMEM((3, size, size), BF16),
                pltpu.SemaphoreType.DMA((2,)),
                pltpu.SemaphoreType.DMA,
                pltpu.SemaphoreType.DMA,
                pltpu.SemaphoreType.DMA((2,)),
                pltpu.SemaphoreType.DMA((2,)),
                pltpu.SemaphoreType.DMA((4,)),
            ],
            compiler_params=pltpu.CompilerParams(collective_id=0, has_side_effects=True),
            name="polarization",
        )(greens.reshape(4, size, size), coulomb.reshape(3, size, size), pattern, jnp.asarray(forward), jnp.asarray(inverse))

    return jax.shard_map(
        local,
        mesh=mesh,
        in_specs=(P(None, None, "energy", "space", None), P(None, "space", None), P("space", None)),
        out_specs=(P(None, None, None, "energy", "space", None), P(None, None, "energy", "space", None)),
        check_vma=False,
    )
```

time: 117 us -> 45.9 us (0.39)
  the two profiles are of different devices: /device:TPU:512 before, /device:TPU:1 now
where the time goes in v1:
time: 45.9 us; the launch traced here: 45.8 us
  Pallas kernels  42.7 us (93%)
  local copies, waits for them, and re-layouts  2.37 us (5%)
  between operations  0.65 us (1%)
    pallas_call x1, Pallas kernels, local(): pl.pallas_call(lambda *refs: kernel(n_energy, n_space, *refs), out_shape=...  42.7 us
    unnamed x4, local copies, waits for them, and re-layouts  2.37 us

profile of v1, /device:TPU:1, one launch (start us, length us, event | category | flops | bytes accessed | tf_op | source)
XLA Modules:
  0.0 45.8 jit_solution(17412871854736516157)
XLA Ops:
  0.6 42.7 %polarization.1 = (bf16[2,2,2,1,128,128]{5,4,3,2,1,0:T(8,128)(2,1)}, bf16[2,2,1,128,128]{4,3,2,1,0:T(8,128)(2,1)}) custom-call(bf16[4,128,128]{2,1,0:T(8,128)(2,1)} %bitcast.1, bf16[3,128,128]{2,1,0:T(8,128)(2,1)} %refs_1_.1, s32[1,2]{1,0:T(1,128)} %refs_2_.1, bf16[512,256]{1,0:T(8,128)(2,1)} %constant.4.clone.refs_3_, bf16[512,512]{1,0:T(8,128)(2,1)} %constant.5.clone.refs_4_), custom_call_target="tpu_custom_call" | custom-call | tf_op jit(solution)/shard_map/polarization/pallas_call | solution.py:170
  43.4 0.0 copy-start
  43.4 1.7 %copy.9 = bf16[2,2,2,1,128,128]{5,4,3,2,1,0:T(8,128)(2,1)} copy(bf16[2,2,2,1,128,128]{5,4,3,2,1,0:T(8,128)(2,1)} %get-tuple-element.4) | data formatting | bytes 524288
  45.1 0.0 copy-done
  45.1 0.7 %copy.10 = bf16[2,2,1,128,128]{4,3,2,1,0:T(8,128)(2,1)} copy(bf16[2,2,1,128,128]{4,3,2,1,0:T(8,128)(2,1)S(1)} %copy-done) | data formatting | bytes 262144
Async XLA Ops:
  43.4 1.7 %copy-start = (bf16[2,2,1,128,128]{4,3,2,1,0:T(8,128)(2,1)S(1)}, bf16[2,2,1,128,128]{4,3,2,1,0:T(8,128)(2,1)}, u32[]{:S(2)}) copy-start(bf16[2,2,1,128,128]{4,3,2,1,0:T(8,128)(2,1)} %get-tuple-element.5) | copy-start | bytes 393220

commit v2 on v1

v2 whole, which is shorter than its diff:
```python
import math

import jax
import jax.numpy as jnp
import numpy as np
from jax import lax
from jax.experimental import pallas as pl
from jax.experimental.pallas import tpu as pltpu
from jax.sharding import PartitionSpec as P

MESH = pl.DeviceIdType.MESH
BF16 = jnp.bfloat16


def make_tables(energies, rows):
    period = 2 * energies
    phases = (np.arange(period)[:, None] * np.arange(energies)[None, :] % period) * (2.0 * math.pi / period)
    cos_part, sin_part = np.cos(phases), np.sin(phases)
    forward = np.block([[cos_part, sin_part], [-sin_part, cos_part]])
    cos_back, sin_back = cos_part.T, sin_part.T
    inverse = np.block(
        [[cos_back, -sin_back], [sin_back, cos_back], [-cos_back, -sin_back], [-sin_back, cos_back]]
    ) * (1.0 / (period * math.sqrt(energies)))
    unit = np.eye(rows)
    return tuple(np.kron(table, unit).astype(np.float32).astype(BF16) for table in (forward, inverse))


def exchange_kernel(
    n_energy, n_space, rows,
    greens, forward, inverse,
    polar,
    gathered, spectra, fwd, inv,
    gather_send, gather_sem, return_send, return_sem, x_send, x_sem, z_send, z_sem, local_sem,
):
    e = lax.axis_index("energy")
    s = lax.axis_index("space")
    n_y = n_energy // 4
    core, x, y = e % 2, (e // 2) % 2, e // 4
    high, z = s % 2, s // 2
    n_z = n_space // 2
    mine = e // 2
    partner = s + 1 - 2 * high
    z_to, z_from = s + 2 - 4 * high, s - 2 + 4 * high
    relays = jnp.where(high == 0, z < n_z - 1, z > 0)
    receives = jnp.where(high == 0, z > 0, z < n_z - 1)
    distances = [n_y // 2]
    for d in range(n_y // 2 - 1, 0, -1):
        distances += [d, -d]

    def part(ref, index):
        return ref.at[:, :, pl.ds(pl.multiple_of(index * rows, rows), rows), :]

    def strip(ref, y_from):
        return ref.at[:, :, pl.ds(pl.multiple_of(y_from * 2 * rows, 2 * rows), 2 * rows), :]

    def at_distance(d):
        return (y + d + n_y) % n_y

    @pl.when(core == 1)
    def _():
        pltpu.make_async_copy(forward, fwd, local_sem.at[0]).start()
        pltpu.make_async_copy(inverse, inv, local_sem.at[1]).start()

    barrier = pltpu.get_barrier_semaphore()
    pl.semaphore_signal(barrier, inc=1, device_id={"space": partner}, device_id_type=MESH)

    @pl.when(receives)
    def _():
        pl.semaphore_signal(barrier, inc=1, device_id={"space": z_from}, device_id_type=MESH)

    @pl.when(core == 1)
    def _():
        def greet(k, carry):
            pl.semaphore_signal(barrier, inc=1, device_id={"energy": (e + k) % n_energy}, device_id_type=MESH)
            return carry

        lax.fori_loop(1, n_energy, greet, 0)

    pl.semaphore_wait(barrier, n_energy // 2 + 1 - core + jnp.where(relays, 1, 0))

    def give(to):
        pltpu.make_async_remote_copy(
            src_ref=part(greens, to),
            dst_ref=part(gathered, e),
            send_sem=gather_send,
            recv_sem=gather_sem,
            device_id={"energy": 2 * to + 1},
            device_id_type=MESH,
        ).start()

    for d in distances:
        for across in (1, 0):
            give(2 * at_distance(d) + (x + across) % 2)
    give(2 * y + 1 - x)

    @pl.when(core == 0)
    def _():
        give(mine)

    @pl.when(jnp.logical_not(receives))
    def _():
        polar[2] = jnp.zeros(polar.shape[1:], BF16)

    @pl.when(core == 1)
    def _():
        own = pltpu.make_async_copy(part(greens, mine), part(gathered, e), local_sem.at[2])
        own.start()
        pltpu.make_async_copy(forward, fwd, local_sem.at[0]).wait()
        pltpu.make_async_copy(inverse, inv, local_sem.at[1]).wait()
        own.wait()
        others = gathered.at[:, :, pl.ds(0, (n_energy - 1) * rows), :]
        pltpu.make_async_copy(others, others, gather_sem).wait()

        size = gathered.shape[-1]
        half = 2 * size
        stacked = jnp.concatenate(
            [
                jnp.concatenate([gathered[2 * a, h], gathered[2 * a + 1, h]], axis=0)
                for a in range(2)
                for h in range(2)
            ],
            axis=1,
        )
        fields = jnp.dot(fwd[...], stacked, preferred_element_type=jnp.float32)
        less_re, less_im = fields[:half, :half], fields[half:, :half]
        great_re, great_im = fields[:half, half:], fields[half:, half:]
        product = jnp.concatenate(
            [less_re * great_im - less_im * great_re, less_re * great_re + less_im * great_im], axis=0
        ).astype(BF16)
        result = jnp.dot(inv[...], product, preferred_element_type=jnp.float32).astype(BF16)
        for i in range(4):
            for h in range(2):
                spectra[i, h] = result[i * size:(i + 1) * size, h * size:(h + 1) * size]

        def give_back(to):
            pltpu.make_async_remote_copy(
                src_ref=part(spectra, to),
                dst_ref=part(polar.at[0], mine),
                send_sem=return_send,
                recv_sem=return_sem.at[y],
                device_id={"energy": to},
                device_id_type=MESH,
            ).start()

        for d in distances:
            for across in (1, 0):
                for c in (0, 1):
                    give_back(4 * at_distance(d) + 2 * ((x + across) % 2) + c)
        for c in (0, 1):
            give_back(4 * y + 2 * (1 - x) + c)
        give_back(e - 1)
        keep = pltpu.make_async_copy(part(spectra, e), part(polar.at[0], mine), local_sem.at[2])
        keep.start()
        keep.wait()

    def hop(y_from):
        return pltpu.make_async_remote_copy(
            src_ref=strip(polar.at[0], y_from),
            dst_ref=strip(polar.at[1], y_from),
            send_sem=x_send,
            recv_sem=x_sem.at[y_from],
            device_id={"space": partner},
            device_id_type=MESH,
        )

    def relay(y_from):
        return pltpu.make_async_remote_copy(
            src_ref=strip(polar.at[1], y_from),
            dst_ref=strip(polar.at[2], y_from),
            send_sem=z_send,
            recv_sem=z_sem.at[y_from],
            device_id={"space": z_to},
            device_id_type=MESH,
        )

    order = [y] + [at_distance(d) for d in distances[::-1]]
    one = part(polar.at[0], 0)
    for y_from in order:
        landed = strip(polar.at[0], y_from)
        if y_from is y:
            @pl.when(core == 0)
            def _():
                pltpu.make_async_copy(landed, landed, return_sem.at[y]).wait()

            @pl.when(core == 1)
            def _():
                pltpu.make_async_copy(one, one, return_sem.at[y]).wait()
        else:
            pltpu.make_async_copy(landed, landed, return_sem.at[y_from]).wait()
        hop(y_from).start()

    for y_from in order:
        hop(y_from).wait_recv()

        @pl.when(relays)
        def _():
            relay(y_from).start()

    @pl.when(receives)
    def _():
        for y_from in order:
            relay(y_from).wait_recv()

    sent = gathered.at[:, :, pl.ds(0, (n_energy // 2 - 1) * rows), :]
    pltpu.make_async_copy(sent, sent, gather_send).wait()

    @pl.when(core == 0)
    def _():
        pltpu.make_async_copy(one, one, gather_send).wait()

    @pl.when(core == 1)
    def _():
        back = spectra.at[:, :, pl.ds(0, (n_energy - 1) * rows), :]
        pltpu.make_async_copy(back, back, return_send).wait()

    pltpu.make_async_copy(polar.at[0], polar.at[0], x_send).wait()

    @pl.when(relays)
    def _():
        pltpu.make_async_copy(polar.at[0], polar.at[0], z_send).wait()


def product_kernel(n_space, polar, coulomb, pattern, sides, screened, out_sides, out_screened, out_sem):
    size = coulomb.shape[-1]
    s = lax.axis_index("space")
    high = s % 2

    def coupling(upper):
        present = jnp.where(jnp.where(upper == 1, s < n_space - 1, s > 0), pattern[0, upper], 0)
        return (coulomb[2 * upper].astype(jnp.float32) * present.astype(jnp.float32)).astype(BF16)

    def image(weight, slot):
        wide = jnp.concatenate([polar[slot, i].reshape(size, size) for i in range(4)], axis=1)
        return jnp.dot(weight, wide, preferred_element_type=jnp.float32).astype(BF16)

    weights = (coulomb[1], coupling(1 - high), coupling(high))
    images = [image(weight, slot) for slot, weight in enumerate(weights)]
    copies = []
    for slot, block in ((1, 1 - high), (2, high)):
        for i in range(4):
            out_sides[slot - 1, i] = images[slot][:, i * size:(i + 1) * size]
        for kind in range(2):
            copies.append(
                pltpu.make_async_copy(
                    out_sides.at[slot - 1, pl.ds(2 * kind, 2)], sides.at[kind, block], out_sem.at[len(copies)]
                )
            )
            copies[-1].start()
    joined_weights = jnp.concatenate(weights, axis=1)
    for i in range(4):
        joined = jnp.concatenate([part[:, i * size:(i + 1) * size] for part in images], axis=1)
        out_screened[i] = lax.dot_general(
            joined, joined_weights, (((1,), (1,)), ((), ())), preferred_element_type=jnp.float32
        ).astype(BF16)
    copies.append(pltpu.make_async_copy(out_screened, screened, out_sem.at[len(copies)]))
    copies[-1].start()
    for copy in copies:
        copy.wait()


def solution(mesh):
    n_energy, n_space = mesh.shape["energy"], mesh.shape["space"]

    def local(greens, coulomb, pattern):
        size = greens.shape[-1]
        rows = size // n_energy
        forward, inverse = make_tables(n_energy, rows)
        anywhere = pl.BlockSpec(memory_space=pl.ANY)
        vmem = pl.BlockSpec(memory_space=pltpu.VMEM)
        dma = pltpu.SemaphoreType.DMA
        strips = n_energy // 4
        polar = pl.pallas_call(
            lambda *refs: exchange_kernel(n_energy, n_space, rows, *refs),
            out_shape=pltpu.VMEM((3, 4, 2, size // 2, size), BF16),
            in_specs=[anywhere] * 3,
            out_specs=vmem,
            scratch_shapes=[
                pltpu.VMEM((4, 2, size, size), BF16),
                pltpu.VMEM((4, 2, size, size), BF16),
                pltpu.VMEM(forward.shape, BF16),
                pltpu.VMEM(inverse.shape, BF16),
                dma, dma, dma, dma((strips,)), dma, dma((strips,)), dma, dma((strips,)), dma((3,)),
            ],
            compiler_params=pltpu.CompilerParams(collective_id=0, has_side_effects=True),
            name="exchange",
        )(greens.reshape(4, 2, size // 2, size), jnp.asarray(forward), jnp.asarray(inverse))
        sides, screened = pl.pallas_call(
            lambda *refs: product_kernel(n_space, *refs),
            out_shape=(
                jax.ShapeDtypeStruct((2, 2, 2, size, size), BF16),
                jax.ShapeDtypeStruct((4, size, size), BF16),
            ),
            in_specs=[vmem, vmem, pl.BlockSpec(memory_space=pltpu.SMEM)],
            out_specs=(anywhere, anywhere),
            scratch_shapes=[
                pltpu.VMEM((2, 4, size, size), BF16),
                pltpu.VMEM((4, size, size), BF16),
                dma((5,)),
            ],
            compiler_params=pltpu.CompilerParams(vmem_limit_bytes=16 << 20),
            name="products",
        )(polar, coulomb.reshape(3, size, size), pattern)
        return sides.reshape(2, 2, 2, 1, size, size), screened.reshape(2, 2, 1, size, size)

    return jax.shard_map(
        local,
        mesh=mesh,
        in_specs=(P(None, None, "energy", "space", None), P(None, "space", None), P("space", None)),
        out_specs=(P(None, None, None, "energy", "space", None), P(None, None, "energy", "space", None)),
        check_vma=False,
    )
```

time: 45.9 us -> 31.5 us (0.69)
  the two profiles are of different devices: /device:TPU:1 before, /device:TPU:512 now
where the time goes in v2:
time: 31.5 us; the launch traced here: 31.4 us
  Pallas kernels  30.7 us (97%)
  between operations  0.67 us (2%)
    pallas_call x1, Pallas kernels, local(): pl.pallas_call(lambda *refs: exchange_kernel(n_energy, n_space, rows, *re...  29 us
    pallas_call x1, Pallas kernels, local(): pl.pallas_call(lambda *refs: product_kernel(n_space, *refs), out_shape=(j...  1.7 us

profile of v2, /device:TPU:512, one launch (start us, length us, event | category | flops | bytes accessed | tf_op | source)
XLA Modules:
  0.0 31.4 jit_solution(4914704685687350801)
XLA Ops:
  0.6 0.0 copy-start
  0.6 0.0 copy-start.1
  0.6 29.0 %exchange.1.refs_0_ = bf16[3,4,2,64,128]{4,3,2,1,0:T(8,128)(2,1)S(1)} custom-call(bf16[4,2,64,128]{3,2,1,0:T(8,128)(2,1)} %bitcast.7, bf16[512,256]{1,0:T(8,128)(2,1)} %constant.4.clone.refs_1_, bf16[512,512]{1,0:T(8,128)(2,1)} %constant.5.clone.refs_2_), custom_call_target="tpu_custom_call" | custom-call | tf_op jit(solution)/shard_map/exchange/pallas_call | solution.py:272
  29.7 0.0 copy-done
  29.7 0.0 copy-done.1
  29.7 1.7 %products.1 = (bf16[2,2,2,128,128]{4,3,2,1,0:T(8,128)(2,1)}, bf16[4,128,128]{2,1,0:T(8,128)(2,1)}) custom-call(bf16[3,4,2,64,128]{4,3,2,1,0:T(8,128)(2,1)S(1)} %exchange.1.refs_0_, bf16[3,128,128]{2,1,0:T(8,128)(2,1)S(1)} %copy-done, s32[1,2]{1,0:T(1,128)S(1)} %copy-done.1), custom_call_target="tpu_custom_call" | custom-call | tf_op jit(solution)/shard_map/products/pallas_call | solution.py:287
Async XLA Ops:
  0.6 29.0 %copy-start = (bf16[3,128,128]{2,1,0:T(8,128)(2,1)S(1)}, bf16[3,128,128]{2,1,0:T(8,128)(2,1)}, u32[]{:S(2)}) copy-start(bf16[3,128,128]{2,1,0:T(8,128)(2,1)} %refs_1_.2) | copy-start | bytes 294916
  0.6 29.0 %copy-start.1 = (s32[1,2]{1,0:T(1,128)S(1)}, s32[1,2]{1,0:T(1,128)}, u32[]{:S(2)}) copy-start(s32[1,2]{1,0:T(1,128)} %refs_2_.2) | copy-start | bytes 28

commit v3 on v2

--- a/solution.py
+++ b/solution.py
@@ -10,6 +10,7 @@
 
 MESH = pl.DeviceIdType.MESH
 BF16 = jnp.bfloat16
+DIRECT = 5
 
 
 def make_tables(energies, rows):
@@ -29,8 +30,8 @@
     n_energy, n_space, rows,
     greens, forward, inverse,
     polar,
-    gathered, spectra, fwd, inv,
-    gather_send, gather_sem, return_send, return_sem, x_send, x_sem, z_send, z_sem, local_sem,
+    gathered, spectra, staged, fwd, inv,
+    gather_send, gather_sem, stage_send, stage_sem, own_send, own_sem, x_send, x_sem, z_send, z_sem, diag_send, local_sem,
 ):
     e = lax.axis_index("energy")
     s = lax.axis_index("space")
@@ -41,11 +42,14 @@
     mine = e // 2
     partner = s + 1 - 2 * high
     z_to, z_from = s + 2 - 4 * high, s - 2 + 4 * high
+    diagonal = s - 1 + 2 * high
     relays = jnp.where(high == 0, z < n_z - 1, z > 0)
     receives = jnp.where(high == 0, z > 0, z < n_z - 1)
-    distances = [n_y // 2]
-    for d in range(n_y // 2 - 1, 0, -1):
-        distances += [d, -d]
+    near = []
+    for d in range(1, n_y // 2):
+        near += [d, -d]
+    near.append(n_y // 2)
+    far = near[::-1]
 
     def part(ref, index):
         return ref.at[:, :, pl.ds(pl.multiple_of(index * rows, rows), rows), :]
@@ -56,27 +60,46 @@
     def at_distance(d):
         return (y + d + n_y) % n_y
 
+    def device(y_to, x_to, core_to):
+        return 4 * y_to + 2 * x_to + core_to
+
+    barrier = pltpu.get_barrier_semaphore()
+
+    @pl.when(core == 1)
+    def _():
+        def greet(to):
+            pl.semaphore_signal(barrier, inc=1, device_id={"energy": to}, device_id_type=MESH)
+
+        for d in far:
+            for x_to in range(2):
+                for c in range(2):
+                    greet(device(at_distance(d), x_to, c))
+        greet(device(y, 1 - x, 0))
+        greet(device(y, 1 - x, 1))
+        greet(e - 1)
+
+    for x_to in range(2):
+        pl.semaphore_signal(
+            barrier, inc=1, device_id={"energy": device(y, x_to, 1), "space": partner}, device_id_type=MESH
+        )
+
+    @pl.when(receives)
+    def _():
+        pl.semaphore_signal(barrier, inc=1, device_id={"space": z_from}, device_id_type=MESH)
+        for x_to in range(2):
+            pl.semaphore_signal(
+                barrier, inc=1, device_id={"energy": device(y, x_to, 1), "space": diagonal}, device_id_type=MESH
+            )
+
     @pl.when(core == 1)
     def _():
         pltpu.make_async_copy(forward, fwd, local_sem.at[0]).start()
         pltpu.make_async_copy(inverse, inv, local_sem.at[1]).start()
 
-    barrier = pltpu.get_barrier_semaphore()
-    pl.semaphore_signal(barrier, inc=1, device_id={"space": partner}, device_id_type=MESH)
-
-    @pl.when(receives)
-    def _():
-        pl.semaphore_signal(barrier, inc=1, device_id={"space": z_from}, device_id_type=MESH)
-
-    @pl.when(core == 1)
-    def _():
-        def greet(k, carry):
-            pl.semaphore_signal(barrier, inc=1, device_id={"energy": (e + k) % n_energy}, device_id_type=MESH)
-            return carry
-
-        lax.fori_loop(1, n_energy, greet, 0)
-
-    pl.semaphore_wait(barrier, n_energy // 2 + 1 - core + jnp.where(relays, 1, 0))
+    pl.semaphore_wait(
+        barrier,
+        n_energy // 2 + 3 * core + jnp.where(relays, 1, 0) + jnp.where(receives, 4 * core, 0),
+    )
 
     def give(to):
         pltpu.make_async_remote_copy(
@@ -88,7 +111,7 @@
             device_id_type=MESH,
         ).start()
 
-    for d in distances:
+    for d in far:
         for across in (1, 0):
             give(2 * at_distance(d) + (x + across) % 2)
     give(2 * y + 1 - x)
@@ -100,6 +123,56 @@
     @pl.when(jnp.logical_not(receives))
     def _():
         polar[2] = jnp.zeros(polar.shape[1:], BF16)
+
+    def stage(y_from, y_to):
+        block = 4 * rows
+        return pltpu.make_async_remote_copy(
+            src_ref=spectra.at[:, :, pl.ds(pl.multiple_of(y_to * block, block), block), :],
+            dst_ref=staged.at[y_from],
+            send_sem=stage_send,
+            recv_sem=stage_sem.at[y_from],
+            device_id={"energy": device(y_to, x, 1)},
+            device_id_type=MESH,
+        )
+
+    def hand_out(y_from, piece, direct):
+        index = 2 * y_from + x
+        if direct:
+            @pl.when(receives)
+            def _():
+                for x_to in range(2):
+                    for c in range(2):
+                        pltpu.make_async_remote_copy(
+                            src_ref=piece(2 * x_to + c),
+                            dst_ref=part(polar.at[2], index),
+                            send_sem=diag_send,
+                            recv_sem=z_sem.at[y_from],
+                            device_id={"energy": device(y, x_to, c), "space": diagonal},
+                            device_id_type=MESH,
+                        ).start()
+
+        for across in (0, 1):
+            for c in (0, 1):
+                x_to = (x + across) % 2
+                pltpu.make_async_remote_copy(
+                    src_ref=piece(2 * x_to + c),
+                    dst_ref=part(polar.at[1], index),
+                    send_sem=x_send,
+                    recv_sem=x_sem.at[y_from],
+                    device_id={"energy": device(y, x_to, c), "space": partner},
+                    device_id_type=MESH,
+                ).start()
+        for across, c in ((1, 0), (1, 1), (0, 0)):
+            x_to = (x + across) % 2
+            pltpu.make_async_remote_copy(
+                src_ref=piece(2 * x_to + c),
+                dst_ref=part(polar.at[0], index),
+                send_sem=own_send,
+                recv_sem=own_sem,
+                device_id={"energy": device(y, x_to, c)},
+                device_id_type=MESH,
+            ).start()
+        pltpu.make_async_copy(piece(2 * x + 1), part(polar.at[0], index), local_sem.at[2]).start()
 
     @pl.when(core == 1)
     def _():
@@ -132,36 +205,13 @@
             for h in range(2):
                 spectra[i, h] = result[i * size:(i + 1) * size, h * size:(h + 1) * size]
 
-        def give_back(to):
-            pltpu.make_async_remote_copy(
-                src_ref=part(spectra, to),
-                dst_ref=part(polar.at[0], mine),
-                send_sem=return_send,
-                recv_sem=return_sem.at[y],
-                device_id={"energy": to},
-                device_id_type=MESH,
-            ).start()
-
-        for d in distances:
-            for across in (1, 0):
-                for c in (0, 1):
-                    give_back(4 * at_distance(d) + 2 * ((x + across) % 2) + c)
-        for c in (0, 1):
-            give_back(4 * y + 2 * (1 - x) + c)
-        give_back(e - 1)
-        keep = pltpu.make_async_copy(part(spectra, e), part(polar.at[0], mine), local_sem.at[2])
-        keep.start()
-        keep.wait()
-
-    def hop(y_from):
-        return pltpu.make_async_remote_copy(
-            src_ref=strip(polar.at[0], y_from),
-            dst_ref=strip(polar.at[1], y_from),
-            send_sem=x_send,
-            recv_sem=x_sem.at[y_from],
-            device_id={"space": partner},
-            device_id_type=MESH,
-        )
+        for d in far:
+            stage(y, at_distance(d)).start()
+        hand_out(y, lambda j: part(spectra, 4 * y + j), False)
+        for i, d in enumerate(near):
+            y_from = at_distance(d)
+            stage(y_from, y_from).wait_recv()
+            hand_out(y_from, lambda j: staged.at[y_from, :, :, pl.ds(j * rows, rows), :], i >= n_y - 1 - DIRECT)
 
     def relay(y_from):
         return pltpu.make_async_remote_copy(
@@ -173,51 +223,58 @@
             device_id_type=MESH,
         )
 
-    order = [y] + [at_distance(d) for d in distances[::-1]]
-    one = part(polar.at[0], 0)
-    for y_from in order:
-        landed = strip(polar.at[0], y_from)
-        if y_from is y:
-            @pl.when(core == 0)
+    order = [y] + [at_distance(d) for d in near]
+    for i, y_from in enumerate(order):
+        landed = strip(polar.at[1], y_from)
+        pltpu.make_async_copy(landed, landed, x_sem.at[y_from]).wait()
+        if i < n_y - DIRECT:
+            @pl.when(relays)
             def _():
-                pltpu.make_async_copy(landed, landed, return_sem.at[y]).wait()
-
+                relay(y_from).start()
+
+    half_own = polar.at[0, pl.ds(0, 2)]
+
+    @pl.when(core == 0)
+    def _():
+        pltpu.make_async_copy(polar.at[0], polar.at[0], own_sem).wait()
+
+    @pl.when(core == 1)
+    def _():
+        pltpu.make_async_copy(half_own, half_own, own_sem).wait()
+        pltpu.make_async_copy(half_own, half_own, local_sem.at[2]).wait()
+
+    sent = gathered.at[:, :, pl.ds(0, (n_energy // 2 - 1) * rows), :]
+    pltpu.make_async_copy(sent, sent, gather_send).wait()
+
+    @pl.when(core == 0)
+    def _():
+        one = part(polar.at[0], 0)
+        pltpu.make_async_copy(one, one, gather_send).wait()
+
+    @pl.when(core == 1)
+    def _():
+        back = spectra.at[:, :, pl.ds(0, (n_y - 1) * 4 * rows), :]
+        pltpu.make_async_copy(back, back, stage_send).wait()
+        six = staged.at[pl.ds(0, 6)]
+        pltpu.make_async_copy(six, six, own_send).wait()
+        two = polar.at[pl.ds(0, 2)]
+        pltpu.make_async_copy(two, two, x_send).wait()
+
+    @pl.when(relays)
+    def _():
+        relayed = polar.at[1, :, :, pl.ds(0, (n_y - DIRECT) * 2 * rows), :]
+        pltpu.make_async_copy(relayed, relayed, z_send).wait()
+
+    @pl.when(receives)
+    def _():
+        if DIRECT > 0:
             @pl.when(core == 1)
             def _():
-                pltpu.make_async_copy(one, one, return_sem.at[y]).wait()
-        else:
-            pltpu.make_async_copy(landed, landed, return_sem.at[y_from]).wait()
-        hop(y_from).start()
-
-    for y_from in order:
-        hop(y_from).wait_recv()
-
-        @pl.when(relays)
-        def _():
-            relay(y_from).start()
-
-    @pl.when(receives)
-    def _():
+                direct = staged.at[pl.ds(0, DIRECT)]
+                pltpu.make_async_copy(direct, direct, diag_send).wait()
+
         for y_from in order:
             relay(y_from).wait_recv()
-
-    sent = gathered.at[:, :, pl.ds(0, (n_energy // 2 - 1) * rows), :]
-    pltpu.make_async_copy(sent, sent, gather_send).wait()
-
-    @pl.when(core == 0)
-    def _():
-        pltpu.make_async_copy(one, one, gather_send).wait()
-
-    @pl.when(core == 1)
-    def _():
-        back = spectra.at[:, :, pl.ds(0, (n_energy - 1) * rows), :]
-        pltpu.make_async_copy(back, back, return_send).wait()
-
-    pltpu.make_async_copy(polar.at[0], polar.at[0], x_send).wait()
-
-    @pl.when(relays)
-    def _():
-        pltpu.make_async_copy(polar.at[0], polar.at[0], z_send).wait()
 
 
 def product_kernel(n_space, polar, coulomb, pattern, sides, screened, out_sides, out_screened, out_sem):
@@ -277,9 +334,10 @@
             scratch_shapes=[
                 pltpu.VMEM((4, 2, size, size), BF16),
                 pltpu.VMEM((4, 2, size, size), BF16),
+                pltpu.VMEM((strips, 4, 2, 4 * rows, size), BF16),
                 pltpu.VMEM(forward.shape, BF16),
                 pltpu.VMEM(inverse.shape, BF16),
-                dma, dma, dma, dma((strips,)), dma, dma((strips,)), dma, dma((strips,)), dma((3,)),
+                dma, dma, dma, dma((strips,)), dma, dma, dma, dma((strips,)), dma, dma((strips,)), dma, dma((3,)),
             ],
             compiler_params=pltpu.CompilerParams(collective_id=0, has_side_effects=True),
             name="exchange",

time: 31.5 us -> 29.1 us (0.924)
  the two profiles are of different devices: /device:TPU:512 before, /device:TPU:1 now
where the time goes in v3:
time: 29.1 us; the launch traced here: 29 us
  Pallas kernels  28.3 us (97%)
  between operations  0.67 us (2%)
    pallas_call x1, Pallas kernels, local(): pl.pallas_call(lambda *refs: exchange_kernel(n_energy, n_space, rows, *re...  26.6 us
    pallas_call x1, Pallas kernels, local(): pl.pallas_call(lambda *refs: product_kernel(n_space, *refs), out_shape=(j...  1.7 us

profile of v3, /device:TPU:1, one launch (start us, length us, event | category | flops | bytes accessed | tf_op | source)
XLA Modules:
  0.0 29.0 jit_solution(3682730191997999766)
XLA Ops:
  0.6 0.0 copy-start
  0.6 0.0 copy-start.1
  0.6 26.6 %exchange.1.refs_0_ = bf16[3,4,2,64,128]{4,3,2,1,0:T(8,128)(2,1)S(1)} custom-call(bf16[4,2,64,128]{3,2,1,0:T(8,128)(2,1)} %bitcast.7, bf16[512,256]{1,0:T(8,128)(2,1)} %constant.4.clone.refs_1_, bf16[512,512]{1,0:T(8,128)(2,1)} %constant.5.clone.refs_2_), custom_call_target="tpu_custom_call" | custom-call | tf_op jit(solution)/shard_map/exchange/pallas_call | solution.py:329
  27.3 0.0 copy-done
  27.3 0.0 copy-done.1
  27.3 1.7 %products.1 = (bf16[2,2,2,128,128]{4,3,2,1,0:T(8,128)(2,1)}, bf16[4,128,128]{2,1,0:T(8,128)(2,1)}) custom-call(bf16[3,4,2,64,128]{4,3,2,1,0:T(8,128)(2,1)S(1)} %exchange.1.refs_0_, bf16[3,128,128]{2,1,0:T(8,128)(2,1)S(1)} %copy-done, s32[1,2]{1,0:T(1,128)S(1)} %copy-done.1), custom_call_target="tpu_custom_call" | custom-call | tf_op jit(solution)/shard_map/products/pallas_call | solution.py:345
Async XLA Ops:
  0.6 26.6 %copy-start = (bf16[3,128,128]{2,1,0:T(8,128)(2,1)S(1)}, bf16[3,128,128]{2,1,0:T(8,128)(2,1)}, u32[]{:S(2)}) copy-start(bf16[3,128,128]{2,1,0:T(8,128)(2,1)} %refs_1_.2) | copy-start | bytes 294916
  0.6 26.6 %copy-start.1 = (s32[1,2]{1,0:T(1,128)S(1)}, s32[1,2]{1,0:T(1,128)}, u32[]{:S(2)}) copy-start(s32[1,2]{1,0:T(1,128)} %refs_2_.2) | copy-start | bytes 28

commit v4 on v3

--- a/solution.py
+++ b/solution.py
@@ -31,7 +31,7 @@
     greens, forward, inverse,
     polar,
     gathered, spectra, staged, fwd, inv,
-    gather_send, gather_sem, stage_send, stage_sem, own_send, own_sem, x_send, x_sem, z_send, z_sem, diag_send, local_sem,
+    gather_send, gather_sem, stage_send, stage_sem, own_send, own_sem, x_send, x_sem, z_send, z_sem, diag_send, local_sem, x_open, z_open,
 ):
     e = lax.axis_index("energy")
     s = lax.axis_index("space")
@@ -77,19 +77,15 @@
         greet(device(y, 1 - x, 0))
         greet(device(y, 1 - x, 1))
         greet(e - 1)
-
-    for x_to in range(2):
-        pl.semaphore_signal(
-            barrier, inc=1, device_id={"energy": device(y, x_to, 1), "space": partner}, device_id_type=MESH
-        )
+        pl.semaphore_signal(barrier, inc=1, device_id={"space": partner}, device_id_type=MESH)
+
+        @pl.when(receives)
+        def _():
+            pl.semaphore_signal(barrier, inc=1, device_id={"space": diagonal}, device_id_type=MESH)
 
     @pl.when(receives)
     def _():
         pl.semaphore_signal(barrier, inc=1, device_id={"space": z_from}, device_id_type=MESH)
-        for x_to in range(2):
-            pl.semaphore_signal(
-                barrier, inc=1, device_id={"energy": device(y, x_to, 1), "space": diagonal}, device_id_type=MESH
-            )
 
     @pl.when(core == 1)
     def _():
@@ -98,7 +94,7 @@
 
     pl.semaphore_wait(
         barrier,
-        n_energy // 2 + 3 * core + jnp.where(relays, 1, 0) + jnp.where(receives, 4 * core, 0),
+        n_energy // 2 + jnp.where(relays, 1, 0) + jnp.where(receives, core, 0),
     )
 
     def give(to):
@@ -183,6 +179,11 @@
         own.wait()
         others = gathered.at[:, :, pl.ds(0, (n_energy - 1) * rows), :]
         pltpu.make_async_copy(others, others, gather_sem).wait()
+        pl.semaphore_signal(x_open, inc=1, device_id={"space": partner}, device_id_type=MESH)
+
+        @pl.when(receives)
+        def _():
+            pl.semaphore_signal(z_open, inc=1, device_id={"space": diagonal}, device_id_type=MESH)
 
         size = gathered.shape[-1]
         half = 2 * size
@@ -205,8 +206,14 @@
             for h in range(2):
                 spectra[i, h] = result[i * size:(i + 1) * size, h * size:(h + 1) * size]
 
-        for d in far:
+        for d in (1, -1, 2, -2, 4, 3, -3):
             stage(y, at_distance(d)).start()
+        pl.semaphore_wait(x_open, 1)
+
+        @pl.when(receives)
+        def _():
+            pl.semaphore_wait(z_open, 1)
+
         hand_out(y, lambda j: part(spectra, 4 * y + j), False)
         for i, d in enumerate(near):
             y_from = at_distance(d)
@@ -338,6 +345,7 @@
                 pltpu.VMEM(forward.shape, BF16),
                 pltpu.VMEM(inverse.shape, BF16),
                 dma, dma, dma, dma((strips,)), dma, dma, dma, dma((strips,)), dma, dma((strips,)), dma, dma((3,)),
+                pltpu.SemaphoreType.REGULAR, pltpu.SemaphoreType.REGULAR,
             ],
             compiler_params=pltpu.CompilerParams(collective_id=0, has_side_effects=True),
             name="exchange",

time: 29.1 us -> 28.1 us (0.966)
  the two profiles are of different devices: /device:TPU:1 before, /device:TPU:512 now
where the time goes in v4:
time: 28.1 us; the launch traced here: 27.7 us
  Pallas kernels  27 us (96%)
  between operations  0.67 us (2%)
    pallas_call x1, Pallas kernels, local(): pl.pallas_call(lambda *refs: exchange_kernel(n_energy, n_space, rows, *re...  25.3 us
    pallas_call x1, Pallas kernels, local(): pl.pallas_call(lambda *refs: product_kernel(n_space, *refs), out_shape=(j...  1.7 us

profile of v4, /device:TPU:512, one launch (start us, length us, event | category | flops | bytes accessed | tf_op | source)
XLA Modules:
  0.0 27.7 jit_solution(11287375652114124216)
XLA Ops:
  0.6 0.0 copy-start
  0.6 0.0 copy-start.1
  0.6 25.3 %exchange.1.refs_0_ = bf16[3,4,2,64,128]{4,3,2,1,0:T(8,128)(2,1)S(1)} custom-call(bf16[4,2,64,128]{3,2,1,0:T(8,128)(2,1)} %bitcast.7, bf16[512,256]{1,0:T(8,128)(2,1)} %constant.4.clone.refs_1_, bf16[512,512]{1,0:T(8,128)(2,1)} %constant.5.clone.refs_2_), custom_call_target="tpu_custom_call" | custom-call | tf_op jit(solution)/shard_map/exchange/pallas_call | solution.py:336
  26.0 0.0 copy-done
  26.0 0.0 copy-done.1
  26.0 1.7 %products.1 = (bf16[2,2,2,128,128]{4,3,2,1,0:T(8,128)(2,1)}, bf16[4,128,128]{2,1,0:T(8,128)(2,1)}) custom-call(bf16[3,4,2,64,128]{4,3,2,1,0:T(8,128)(2,1)S(1)} %exchange.1.refs_0_, bf16[3,128,128]{2,1,0:T(8,128)(2,1)S(1)} %copy-done, s32[1,2]{1,0:T(1,128)S(1)} %copy-done.1), custom_call_target="tpu_custom_call" | custom-call | tf_op jit(solution)/shard_map/products/pallas_call | solution.py:353
Async XLA Ops:
  0.6 25.3 %copy-start = (bf16[3,128,128]{2,1,0:T(8,128)(2,1)S(1)}, bf16[3,128,128]{2,1,0:T(8,128)(2,1)}, u32[]{:S(2)}) copy-start(bf16[3,128,128]{2,1,0:T(8,128)(2,1)} %refs_1_.2) | copy-start | bytes 294916
  0.6 25.3 %copy-start.1 = (s32[1,2]{1,0:T(1,128)S(1)}, s32[1,2]{1,0:T(1,128)}, u32[]{:S(2)}) copy-start(s32[1,2]{1,0:T(1,128)} %refs_2_.2) | copy-start | bytes 28

commit v5 on v4

--- a/solution.py
+++ b/solution.py
@@ -10,7 +10,7 @@
 
 MESH = pl.DeviceIdType.MESH
 BF16 = jnp.bfloat16
-DIRECT = 5
+KEEP = 8
 
 
 def make_tables(energies, rows):
@@ -31,7 +31,7 @@
     greens, forward, inverse,
     polar,
     gathered, spectra, staged, fwd, inv,
-    gather_send, gather_sem, stage_send, stage_sem, own_send, own_sem, x_send, x_sem, z_send, z_sem, diag_send, local_sem, x_open, z_open,
+    gather_send, gather_sem, stage_send, stage_sem, own_send, own_sem, x_send, x_sem, z_send, z_sem, local_sem, x_open, z_open,
 ):
     e = lax.axis_index("energy")
     s = lax.axis_index("space")
@@ -41,10 +41,8 @@
     n_z = n_space // 2
     mine = e // 2
     partner = s + 1 - 2 * high
-    z_to, z_from = s + 2 - 4 * high, s - 2 + 4 * high
     diagonal = s - 1 + 2 * high
-    relays = jnp.where(high == 0, z < n_z - 1, z > 0)
-    receives = jnp.where(high == 0, z > 0, z < n_z - 1)
+    reaches = jnp.where(high == 0, z > 0, z < n_z - 1)
     near = []
     for d in range(1, n_y // 2):
         near += [d, -d]
@@ -53,9 +51,6 @@
 
     def part(ref, index):
         return ref.at[:, :, pl.ds(pl.multiple_of(index * rows, rows), rows), :]
-
-    def strip(ref, y_from):
-        return ref.at[:, :, pl.ds(pl.multiple_of(y_from * 2 * rows, 2 * rows), 2 * rows), :]
 
     def at_distance(d):
         return (y + d + n_y) % n_y
@@ -79,13 +74,9 @@
         greet(e - 1)
         pl.semaphore_signal(barrier, inc=1, device_id={"space": partner}, device_id_type=MESH)
 
-        @pl.when(receives)
+        @pl.when(reaches)
         def _():
             pl.semaphore_signal(barrier, inc=1, device_id={"space": diagonal}, device_id_type=MESH)
-
-    @pl.when(receives)
-    def _():
-        pl.semaphore_signal(barrier, inc=1, device_id={"space": z_from}, device_id_type=MESH)
 
     @pl.when(core == 1)
     def _():
@@ -94,7 +85,7 @@
 
     pl.semaphore_wait(
         barrier,
-        n_energy // 2 + jnp.where(relays, 1, 0) + jnp.where(receives, core, 0),
+        n_energy // 2 + jnp.where(reaches, core, 0),
     )
 
     def give(to):
@@ -116,7 +107,7 @@
     def _():
         give(mine)
 
-    @pl.when(jnp.logical_not(receives))
+    @pl.when(jnp.logical_not(reaches))
     def _():
         polar[2] = jnp.zeros(polar.shape[1:], BF16)
 
@@ -131,33 +122,30 @@
             device_id_type=MESH,
         )
 
-    def hand_out(y_from, piece, direct):
+    def pass_on(y_from, piece):
         index = 2 * y_from + x
-        if direct:
-            @pl.when(receives)
-            def _():
-                for x_to in range(2):
-                    for c in range(2):
-                        pltpu.make_async_remote_copy(
-                            src_ref=piece(2 * x_to + c),
-                            dst_ref=part(polar.at[2], index),
-                            send_sem=diag_send,
-                            recv_sem=z_sem.at[y_from],
-                            device_id={"energy": device(y, x_to, c), "space": diagonal},
-                            device_id_type=MESH,
-                        ).start()
-
-        for across in (0, 1):
-            for c in (0, 1):
-                x_to = (x + across) % 2
-                pltpu.make_async_remote_copy(
-                    src_ref=piece(2 * x_to + c),
-                    dst_ref=part(polar.at[1], index),
-                    send_sem=x_send,
-                    recv_sem=x_sem.at[y_from],
-                    device_id={"energy": device(y, x_to, c), "space": partner},
-                    device_id_type=MESH,
-                ).start()
+
+        def give_to(slot, row, send, recv):
+            for across in (0, 1):
+                for c in (0, 1):
+                    x_to = (x + across) % 2
+                    pltpu.make_async_remote_copy(
+                        src_ref=piece(2 * x_to + c),
+                        dst_ref=part(polar.at[slot], index),
+                        send_sem=send,
+                        recv_sem=recv,
+                        device_id={"energy": device(y, x_to, c), "space": row},
+                        device_id_type=MESH,
+                    ).start()
+
+        @pl.when(reaches)
+        def _():
+            give_to(2, diagonal, z_send, z_sem)
+
+        give_to(1, partner, x_send, x_sem)
+
+    def hand_out(y_from, piece):
+        index = 2 * y_from + x
         for across, c in ((1, 0), (1, 1), (0, 0)):
             x_to = (x + across) % 2
             pltpu.make_async_remote_copy(
@@ -181,7 +169,7 @@
         pltpu.make_async_copy(others, others, gather_sem).wait()
         pl.semaphore_signal(x_open, inc=1, device_id={"space": partner}, device_id_type=MESH)
 
-        @pl.when(receives)
+        @pl.when(reaches)
         def _():
             pl.semaphore_signal(z_open, inc=1, device_id={"space": diagonal}, device_id_type=MESH)
 
@@ -210,34 +198,22 @@
             stage(y, at_distance(d)).start()
         pl.semaphore_wait(x_open, 1)
 
-        @pl.when(receives)
+        @pl.when(reaches)
         def _():
             pl.semaphore_wait(z_open, 1)
 
-        hand_out(y, lambda j: part(spectra, 4 * y + j), False)
-        for i, d in enumerate(near):
+        pieces = [(y, lambda j: part(spectra, 4 * y + j))]
+        for d in near:
             y_from = at_distance(d)
-            stage(y_from, y_from).wait_recv()
-            hand_out(y_from, lambda j: staged.at[y_from, :, :, pl.ds(j * rows, rows), :], i >= n_y - 1 - DIRECT)
-
-    def relay(y_from):
-        return pltpu.make_async_remote_copy(
-            src_ref=strip(polar.at[1], y_from),
-            dst_ref=strip(polar.at[2], y_from),
-            send_sem=z_send,
-            recv_sem=z_sem.at[y_from],
-            device_id={"space": z_to},
-            device_id_type=MESH,
-        )
-
-    order = [y] + [at_distance(d) for d in near]
-    for i, y_from in enumerate(order):
-        landed = strip(polar.at[1], y_from)
-        pltpu.make_async_copy(landed, landed, x_sem.at[y_from]).wait()
-        if i < n_y - DIRECT:
-            @pl.when(relays)
-            def _():
-                relay(y_from).start()
+            pieces.append((y_from, lambda j, y_from=y_from: staged.at[y_from, :, :, pl.ds(j * rows, rows), :]))
+        for i, (y_from, piece) in enumerate(pieces):
+            if i > 0:
+                stage(y_from, y_from).wait_recv()
+            pass_on(y_from, piece)
+            if i < KEEP:
+                hand_out(y_from, piece)
+        for y_from, piece in pieces[KEEP:]:
+            hand_out(y_from, piece)
 
     half_own = polar.at[0, pl.ds(0, 2)]
 
@@ -264,24 +240,17 @@
         pltpu.make_async_copy(back, back, stage_send).wait()
         six = staged.at[pl.ds(0, 6)]
         pltpu.make_async_copy(six, six, own_send).wait()
-        two = polar.at[pl.ds(0, 2)]
-        pltpu.make_async_copy(two, two, x_send).wait()
-
-    @pl.when(relays)
-    def _():
-        relayed = polar.at[1, :, :, pl.ds(0, (n_y - DIRECT) * 2 * rows), :]
-        pltpu.make_async_copy(relayed, relayed, z_send).wait()
-
-    @pl.when(receives)
-    def _():
-        if DIRECT > 0:
-            @pl.when(core == 1)
-            def _():
-                direct = staged.at[pl.ds(0, DIRECT)]
-                pltpu.make_async_copy(direct, direct, diag_send).wait()
-
-        for y_from in order:
-            relay(y_from).wait_recv()
+        pltpu.make_async_copy(staged, staged, x_send).wait()
+
+        @pl.when(reaches)
+        def _():
+            pltpu.make_async_copy(staged, staged, z_send).wait()
+
+    pltpu.make_async_copy(polar.at[1], polar.at[1], x_sem).wait()
+
+    @pl.when(reaches)
+    def _():
+        pltpu.make_async_copy(polar.at[2], polar.at[2], z_sem).wait()
 
 
 def product_kernel(n_space, polar, coulomb, pattern, sides, screened, out_sides, out_screened, out_sem):
@@ -289,37 +258,44 @@
     s = lax.axis_index("space")
     high = s % 2
 
+    present = pattern[...].astype(jnp.float32)
+    below = present[:, 0:1] * jnp.where(s > 0, 1.0, 0.0)
+    above = present[:, 1:2] * jnp.where(s < n_space - 1, 1.0, 0.0)
+
     def coupling(upper):
-        present = jnp.where(jnp.where(upper == 1, s < n_space - 1, s > 0), pattern[0, upper], 0)
-        return (coulomb[2 * upper].astype(jnp.float32) * present.astype(jnp.float32)).astype(BF16)
+        mark = jnp.where(upper == 1, above, below)
+        return (coulomb[2 * upper].astype(jnp.float32) * mark).astype(BF16)
 
     def image(weight, slot):
         wide = jnp.concatenate([polar[slot, i].reshape(size, size) for i in range(4)], axis=1)
         return jnp.dot(weight, wide, preferred_element_type=jnp.float32).astype(BF16)
 
     weights = (coulomb[1], coupling(1 - high), coupling(high))
-    images = [image(weight, slot) for slot, weight in enumerate(weights)]
     copies = []
+    images = [image(weights[0], 0)]
     for slot, block in ((1, 1 - high), (2, high)):
+        images.append(image(weights[slot], slot))
         for i in range(4):
-            out_sides[slot - 1, i] = images[slot][:, i * size:(i + 1) * size]
-        for kind in range(2):
-            copies.append(
-                pltpu.make_async_copy(
-                    out_sides.at[slot - 1, pl.ds(2 * kind, 2)], sides.at[kind, block], out_sem.at[len(copies)]
-                )
-            )
-            copies[-1].start()
-    joined_weights = jnp.concatenate(weights, axis=1)
+            out_sides[slot - 1, i // 2, i % 2] = images[slot][:, i * size:(i + 1) * size]
+        copies.append(pltpu.make_async_copy(out_sides.at[slot - 1], sides.at[:, block], out_sem.at[slot - 1]))
+    joined = jnp.concatenate(
+        [jnp.concatenate([part[:, i * size:(i + 1) * size] for part in images], axis=1) for i in range(4)], axis=0
+    )
+    result = lax.dot_general(
+        joined,
+        jnp.concatenate(weights, axis=1),
+        (((1,), (1,)), ((), ())),
+        preferred_element_type=jnp.float32,
+    ).astype(BF16)
     for i in range(4):
-        joined = jnp.concatenate([part[:, i * size:(i + 1) * size] for part in images], axis=1)
-        out_screened[i] = lax.dot_general(
-            joined, joined_weights, (((1,), (1,)), ((), ())), preferred_element_type=jnp.float32
-        ).astype(BF16)
-    copies.append(pltpu.make_async_copy(out_screened, screened, out_sem.at[len(copies)]))
-    copies[-1].start()
+        out_screened[i] = result[i * size:(i + 1) * size]
+    last = pltpu.make_async_copy(out_screened, screened, out_sem.at[2])
+    for copy in copies:
+        copy.start()
+    last.start()
     for copy in copies:
         copy.wait()
+    last.wait()
 
 
 def solution(mesh):
@@ -344,7 +320,7 @@
                 pltpu.VMEM((strips, 4, 2, 4 * rows, size), BF16),
                 pltpu.VMEM(forward.shape, BF16),
                 pltpu.VMEM(inverse.shape, BF16),
-                dma, dma, dma, dma((strips,)), dma, dma, dma, dma((strips,)), dma, dma((strips,)), dma, dma((3,)),
+                dma, dma, dma, dma((strips,)), dma, dma, dma, dma, dma, dma, dma((3,)),
                 pltpu.SemaphoreType.REGULAR, pltpu.SemaphoreType.REGULAR,
             ],
             compiler_params=pltpu.CompilerParams(collective_id=0, has_side_effects=True),
@@ -356,12 +332,12 @@
                 jax.ShapeDtypeStruct((2, 2, 2, size, size), BF16),
                 jax.ShapeDtypeStruct((4, size, size), BF16),
             ),
-            in_specs=[vmem, vmem, pl.BlockSpec(memory_space=pltpu.SMEM)],
+            in_specs=[vmem, vmem, vmem],
             out_specs=(anywhere, anywhere),
             scratch_shapes=[
-                pltpu.VMEM((2, 4, size, size), BF16),
+                pltpu.VMEM((2, 2, 2, size, size), BF16),
                 pltpu.VMEM((4, size, size), BF16),
-                dma((5,)),
+                dma((3,)),
             ],
             compiler_params=pltpu.CompilerParams(vmem_limit_bytes=16 << 20),
             name="products",

time: 28.1 us -> 27.5 us (0.979)
  Pallas kernels: 27 us -> 26.4 us
    pallas_call x1, Pallas kernels: 1.7 us -> 1.22 us  [local(): pl.pallas_call(lambda *refs: product_kernel(n_space, *refs), out_shape=(j...]
where the time goes in v5:
time: 27.5 us; the launch traced here: 27.1 us
  Pallas kernels  26.4 us (96%)
  between operations  0.67 us (2%)
    pallas_call x1, Pallas kernels, local(): pl.pallas_call(lambda *refs: exchange_kernel(n_energy, n_space, rows, *re...  25.2 us
    pallas_call x1, Pallas kernels, local(): pl.pallas_call(lambda *refs: product_kernel(n_space, *refs), out_shape=(j...  1.22 us

profile of v5, /device:TPU:512, one launch (start us, length us, event | category | flops | bytes accessed | tf_op | source)
XLA Modules:
  0.0 27.1 jit_solution(17529313281784837002)
XLA Ops:
  0.6 0.0 copy-start
  0.6 0.0 copy-start.1
  0.6 25.2 %exchange.1.refs_0_ = bf16[3,4,2,64,128]{4,3,2,1,0:T(8,128)(2,1)S(1)} custom-call(bf16[4,2,64,128]{3,2,1,0:T(8,128)(2,1)} %bitcast.7, bf16[512,256]{1,0:T(8,128)(2,1)} %constant.4.clone.refs_1_, bf16[512,512]{1,0:T(8,128)(2,1)} %constant.5.clone.refs_2_), custom_call_target="tpu_custom_call" | custom-call | tf_op jit(solution)/shard_map/exchange/pallas_call | solution.py:312
  25.8 0.0 copy-done
  25.8 0.0 copy-done.1
  25.9 1.2 %products.1 = (bf16[2,2,2,128,128]{4,3,2,1,0:T(8,128)(2,1)}, bf16[4,128,128]{2,1,0:T(8,128)(2,1)}) custom-call(bf16[3,4,2,64,128]{4,3,2,1,0:T(8,128)(2,1)S(1)} %exchange.1.refs_0_, bf16[3,128,128]{2,1,0:T(8,128)(2,1)S(1)} %copy-done, s32[1,2]{1,0:T(1,128)S(1)} %copy-done.1), custom_call_target="tpu_custom_call" | custom-call | tf_op jit(solution)/shard_map/products/pallas_call | solution.py:329
Async XLA Ops:
  0.6 25.2 %copy-start = (bf16[3,128,128]{2,1,0:T(8,128)(2,1)S(1)}, bf16[3,128,128]{2,1,0:T(8,128)(2,1)}, u32[]{:S(2)}) copy-start(bf16[3,128,128]{2,1,0:T(8,128)(2,1)} %refs_1_.2) | copy-start | bytes 294916
  0.6 25.2 %copy-start.1 = (s32[1,2]{1,0:T(1,128)S(1)}, s32[1,2]{1,0:T(1,128)}, u32[]{:S(2)}) copy-start(s32[1,2]{1,0:T(1,128)} %refs_2_.2) | copy-start | bytes 28

commit v6 on v5

--- a/solution.py
+++ b/solution.py
@@ -30,7 +30,7 @@
     n_energy, n_space, rows,
     greens, forward, inverse,
     polar,
-    gathered, spectra, staged, fwd, inv,
+    gathered, spectra, staged, fwd, inv, held,
     gather_send, gather_sem, stage_send, stage_sem, own_send, own_sem, x_send, x_sem, z_send, z_sem, local_sem, x_open, z_open,
 ):
     e = lax.axis_index("energy")
@@ -58,6 +58,8 @@
     def device(y_to, x_to, core_to):
         return 4 * y_to + 2 * x_to + core_to
 
+    hold = pltpu.make_async_copy(greens, held, local_sem.at[3])
+    hold.start()
     barrier = pltpu.get_barrier_semaphore()
 
     @pl.when(core == 1)
@@ -88,9 +90,11 @@
         n_energy // 2 + jnp.where(reaches, core, 0),
     )
 
+    hold.wait()
+
     def give(to):
         pltpu.make_async_remote_copy(
-            src_ref=part(greens, to),
+            src_ref=part(held, to),
             dst_ref=part(gathered, e),
             send_sem=gather_send,
             recv_sem=gather_sem,
@@ -160,7 +164,7 @@
 
     @pl.when(core == 1)
     def _():
-        own = pltpu.make_async_copy(part(greens, mine), part(gathered, e), local_sem.at[2])
+        own = pltpu.make_async_copy(part(held, mine), part(gathered, e), local_sem.at[2])
         own.start()
         pltpu.make_async_copy(forward, fwd, local_sem.at[0]).wait()
         pltpu.make_async_copy(inverse, inv, local_sem.at[1]).wait()
@@ -183,12 +187,16 @@
             ],
             axis=1,
         )
-        fields = jnp.dot(fwd[...], stacked, preferred_element_type=jnp.float32)
-        less_re, less_im = fields[:half, :half], fields[half:, :half]
-        great_re, great_im = fields[:half, half:], fields[half:, half:]
-        product = jnp.concatenate(
-            [less_re * great_im - less_im * great_re, less_re * great_re + less_im * great_im], axis=0
-        ).astype(BF16)
+        real_parts, imag_parts = [], []
+        step = half // 2
+        for c in range(2):
+            real = jnp.dot(fwd[c * step:(c + 1) * step], stacked, preferred_element_type=jnp.float32)
+            imag = jnp.dot(fwd[half + c * step:half + (c + 1) * step], stacked, preferred_element_type=jnp.float32)
+            less_re, less_im = real[:, :half], imag[:, :half]
+            great_re, great_im = real[:, half:], imag[:, half:]
+            real_parts.append((less_re * great_im - less_im * great_re).astype(BF16))
+            imag_parts.append((less_re * great_re + less_im * great_im).astype(BF16))
+        product = jnp.concatenate(real_parts + imag_parts, axis=0)
         result = jnp.dot(inv[...], product, preferred_element_type=jnp.float32).astype(BF16)
         for i in range(4):
             for h in range(2):
@@ -320,7 +328,8 @@
                 pltpu.VMEM((strips, 4, 2, 4 * rows, size), BF16),
                 pltpu.VMEM(forward.shape, BF16),
                 pltpu.VMEM(inverse.shape, BF16),
-                dma, dma, dma, dma((strips,)), dma, dma, dma, dma, dma, dma, dma((3,)),
+                pltpu.VMEM((4, 2, size // 2, size), BF16),
+                dma, dma, dma, dma((strips,)), dma, dma, dma, dma, dma, dma, dma((4,)),
                 pltpu.SemaphoreType.REGULAR, pltpu.SemaphoreType.REGULAR,
             ],
             compiler_params=pltpu.CompilerParams(collective_id=0, has_side_effects=True),

time: 27.5 us -> 27.2 us (0.989)
  Pallas kernels: 26.4 us -> 26 us
    pallas_call x1, Pallas kernels: 25.2 us -> 24.8 us  [local(): pl.pallas_call(lambda *refs: exchange_kernel(n_energy, n_space, rows, *re...]
where the time goes in v6:
time: 27.2 us; the launch traced here: 26.7 us
  Pallas kernels  26 us (96%)
  between operations  0.67 us (2%)
    pallas_call x1, Pallas kernels, local(): pl.pallas_call(lambda *refs: exchange_kernel(n_energy, n_space, rows, *re...  24.8 us
    pallas_call x1, Pallas kernels, local(): pl.pallas_call(lambda *refs: product_kernel(n_space, *refs), out_shape=(j...  1.22 us

profile of v6, /device:TPU:512, one launch (start us, length us, event | category | flops | bytes accessed | tf_op | source)
XLA Modules:
  0.0 26.7 jit_solution(12552387927640254219)
XLA Ops:
  0.6 0.0 copy-start
  0.6 0.0 copy-start.1
  0.6 24.8 %exchange.1.refs_0_ = bf16[3,4,2,64,128]{4,3,2,1,0:T(8,128)(2,1)S(1)} custom-call(bf16[4,2,64,128]{3,2,1,0:T(8,128)(2,1)} %bitcast.7, bf16[512,256]{1,0:T(8,128)(2,1)} %constant.4.clone.refs_1_, bf16[512,512]{1,0:T(8,128)(2,1)} %constant.5.clone.refs_2_), custom_call_target="tpu_custom_call" | custom-call | tf_op jit(solution)/shard_map/exchange/pallas_call | solution.py:320
  25.5 0.0 copy-done
  25.5 0.0 copy-done.1
  25.5 1.2 %products.1 = (bf16[2,2,2,128,128]{4,3,2,1,0:T(8,128)(2,1)}, bf16[4,128,128]{2,1,0:T(8,128)(2,1)}) custom-call(bf16[3,4,2,64,128]{4,3,2,1,0:T(8,128)(2,1)S(1)} %exchange.1.refs_0_, bf16[3,128,128]{2,1,0:T(8,128)(2,1)S(1)} %copy-done, s32[1,2]{1,0:T(1,128)S(1)} %copy-done.1), custom_call_target="tpu_custom_call" | custom-call | tf_op jit(solution)/shard_map/products/pallas_call | solution.py:338
Async XLA Ops:
  0.6 24.9 %copy-start = (bf16[3,128,128]{2,1,0:T(8,128)(2,1)S(1)}, bf16[3,128,128]{2,1,0:T(8,128)(2,1)}, u32[]{:S(2)}) copy-start(bf16[3,128,128]{2,1,0:T(8,128)(2,1)} %refs_1_.2) | copy-start | bytes 294916
  0.6 24.9 %copy-start.1 = (s32[1,2]{1,0:T(1,128)S(1)}, s32[1,2]{1,0:T(1,128)}, u32[]{:S(2)}) copy-start(s32[1,2]{1,0:T(1,128)} %refs_2_.2) | copy-start | bytes 28

commit v7 on v6

--- a/solution.py
+++ b/solution.py
@@ -36,10 +36,11 @@
     e = lax.axis_index("energy")
     s = lax.axis_index("space")
     n_y = n_energy // 4
-    core, x, y = e % 2, (e // 2) % 2, e // 4
-    high, z = s % 2, s // 2
+    core, mine, y = lax.rem(e, 2), lax.div(e, 2), lax.div(e, 4)
+    x = mine - 2 * y
+    z = lax.div(s, 2)
+    high = s - 2 * z
     n_z = n_space // 2
-    mine = e // 2
     partner = s + 1 - 2 * high
     diagonal = s - 1 + 2 * high
     reaches = jnp.where(high == 0, z > 0, z < n_z - 1)
@@ -53,7 +54,7 @@
         return ref.at[:, :, pl.ds(pl.multiple_of(index * rows, rows), rows), :]
 
     def at_distance(d):
-        return (y + d + n_y) % n_y
+        return lax.rem(y + (d + n_y) % n_y, n_y)
 
     def device(y_to, x_to, core_to):
         return 4 * y_to + 2 * x_to + core_to
@@ -104,7 +105,7 @@
 
     for d in far:
         for across in (1, 0):
-            give(2 * at_distance(d) + (x + across) % 2)
+            give(2 * at_distance(d) + (1 - x if across else x))
     give(2 * y + 1 - x)
 
     @pl.when(core == 0)
@@ -132,7 +133,7 @@
         def give_to(slot, row, send, recv):
             for across in (0, 1):
                 for c in (0, 1):
-                    x_to = (x + across) % 2
+                    x_to = 1 - x if across else x
                     pltpu.make_async_remote_copy(
                         src_ref=piece(2 * x_to + c),
                         dst_ref=part(polar.at[slot], index),
@@ -151,7 +152,7 @@
     def hand_out(y_from, piece):
         index = 2 * y_from + x
         for across, c in ((1, 0), (1, 1), (0, 0)):
-            x_to = (x + across) % 2
+            x_to = 1 - x if across else x
             pltpu.make_async_remote_copy(
                 src_ref=piece(2 * x_to + c),
                 dst_ref=part(polar.at[0], index),
@@ -217,9 +218,8 @@
         for i, (y_from, piece) in enumerate(pieces):
             if i > 0:
                 stage(y_from, y_from).wait_recv()
+            hand_out(y_from, piece)
             pass_on(y_from, piece)
-            if i < KEEP:
-                hand_out(y_from, piece)
         for y_from, piece in pieces[KEEP:]:
             hand_out(y_from, piece)
 

time: 27.2 us -> 26.9 us (0.989)
    pallas_call x1, Pallas kernels: 24.8 us -> 24.6 us  [local(): pl.pallas_call(lambda *refs: exchange_kernel(n_energy, n_space, rows, *re...]
where the time goes in v7:
time: 26.9 us; the launch traced here: 26.4 us
  Pallas kernels  25.8 us (96%)
  between operations  0.67 us (2%)
    pallas_call x1, Pallas kernels, local(): pl.pallas_call(lambda *refs: exchange_kernel(n_energy, n_space, rows, *re...  24.6 us
    pallas_call x1, Pallas kernels, local(): pl.pallas_call(lambda *refs: product_kernel(n_space, *refs), out_shape=(j...  1.22 us

profile of v7, /device:TPU:512, one launch (start us, length us, event | category | flops | bytes accessed | tf_op | source)
XLA Modules:
  0.0 26.4 jit_solution(2005358844889142303)
XLA Ops:
  0.6 0.0 copy-start
  0.6 0.0 copy-start.1
  0.6 24.6 %exchange.1.refs_0_ = bf16[3,4,2,64,128]{4,3,2,1,0:T(8,128)(2,1)S(1)} custom-call(bf16[4,2,64,128]{3,2,1,0:T(8,128)(2,1)} %bitcast.7, bf16[512,256]{1,0:T(8,128)(2,1)} %constant.4.clone.refs_1_, bf16[512,512]{1,0:T(8,128)(2,1)} %constant.5.clone.refs_2_), custom_call_target="tpu_custom_call" | custom-call | tf_op jit(solution)/shard_map/exchange/pallas_call | solution.py:320
  25.2 0.0 copy-done
  25.2 0.0 copy-done.1
  25.2 1.2 %products.1 = (bf16[2,2,2,128,128]{4,3,2,1,0:T(8,128)(2,1)}, bf16[4,128,128]{2,1,0:T(8,128)(2,1)}) custom-call(bf16[3,4,2,64,128]{4,3,2,1,0:T(8,128)(2,1)S(1)} %exchange.1.refs_0_, bf16[3,128,128]{2,1,0:T(8,128)(2,1)S(1)} %copy-done, s32[1,2]{1,0:T(1,128)S(1)} %copy-done.1), custom_call_target="tpu_custom_call" | custom-call | tf_op jit(solution)/shard_map/products/pallas_call | solution.py:338
Async XLA Ops:
  0.6 24.6 %copy-start = (bf16[3,128,128]{2,1,0:T(8,128)(2,1)S(1)}, bf16[3,128,128]{2,1,0:T(8,128)(2,1)}, u32[]{:S(2)}) copy-start(bf16[3,128,128]{2,1,0:T(8,128)(2,1)} %refs_1_.2) | copy-start | bytes 294916
  0.6 24.6 %copy-start.1 = (s32[1,2]{1,0:T(1,128)S(1)}, s32[1,2]{1,0:T(1,128)}, u32[]{:S(2)}) copy-start(s32[1,2]{1,0:T(1,128)} %refs_2_.2) | copy-start | bytes 28

commit v8 on v7

--- a/solution.py
+++ b/solution.py
@@ -10,7 +10,6 @@
 
 MESH = pl.DeviceIdType.MESH
 BF16 = jnp.bfloat16
-KEEP = 8
 
 
 def make_tables(energies, rows):
@@ -205,12 +204,6 @@
 
         for d in (1, -1, 2, -2, 4, 3, -3):
             stage(y, at_distance(d)).start()
-        pl.semaphore_wait(x_open, 1)
-
-        @pl.when(reaches)
-        def _():
-            pl.semaphore_wait(z_open, 1)
-
         pieces = [(y, lambda j: part(spectra, 4 * y + j))]
         for d in near:
             y_from = at_distance(d)
@@ -219,9 +212,14 @@
             if i > 0:
                 stage(y_from, y_from).wait_recv()
             hand_out(y_from, piece)
+            if i == 0:
+                pl.semaphore_wait(x_open, 1)
+
+                @pl.when(reaches)
+                def _():
+                    pl.semaphore_wait(z_open, 1)
+
             pass_on(y_from, piece)
-        for y_from, piece in pieces[KEEP:]:
-            hand_out(y_from, piece)
 
     half_own = polar.at[0, pl.ds(0, 2)]
 

time: 26.9 us -> 27.2 us (1.011)
  Pallas kernels: 25.8 us -> 26.1 us
    pallas_call x1, Pallas kernels: 24.6 us -> 24.8 us  [local(): pl.pallas_call(lambda *refs: exchange_kernel(n_energy, n_space, rows, *re...]
where the time goes in v8:
time: 27.2 us; the launch traced here: 26.7 us
  Pallas kernels  26.1 us (96%)
  between operations  0.67 us (2%)
    pallas_call x1, Pallas kernels, local(): pl.pallas_call(lambda *refs: exchange_kernel(n_energy, n_space, rows, *re...  24.8 us
    pallas_call x1, Pallas kernels, local(): pl.pallas_call(lambda *refs: product_kernel(n_space, *refs), out_shape=(j...  1.23 us

profile of v8, /device:TPU:512, one launch (start us, length us, event | category | flops | bytes accessed | tf_op | source)
XLA Modules:
  0.0 26.7 jit_solution(8649040850354450654)
XLA Ops:
  0.6 0.0 copy-start
  0.6 0.0 copy-start.1
  0.6 24.8 %exchange.1.refs_0_ = bf16[3,4,2,64,128]{4,3,2,1,0:T(8,128)(2,1)S(1)} custom-call(bf16[4,2,64,128]{3,2,1,0:T(8,128)(2,1)} %bitcast.7, bf16[512,256]{1,0:T(8,128)(2,1)} %constant.4.clone.refs_1_, bf16[512,512]{1,0:T(8,128)(2,1)} %constant.5.clone.refs_2_), custom_call_target="tpu_custom_call" | custom-call | tf_op jit(solution)/shard_map/exchange/pallas_call | solution.py:318
  25.5 0.0 copy-done
  25.5 0.0 copy-done.1
  25.5 1.2 %products.1 = (bf16[2,2,2,128,128]{4,3,2,1,0:T(8,128)(2,1)}, bf16[4,128,128]{2,1,0:T(8,128)(2,1)}) custom-call(bf16[3,4,2,64,128]{4,3,2,1,0:T(8,128)(2,1)S(1)} %exchange.1.refs_0_, bf16[3,128,128]{2,1,0:T(8,128)(2,1)S(1)} %copy-done, s32[1,2]{1,0:T(1,128)S(1)} %copy-done.1), custom_call_target="tpu_custom_call" | custom-call | tf_op jit(solution)/shard_map/products/pallas_call | solution.py:336
Async XLA Ops:
  0.6 24.9 %copy-start = (bf16[3,128,128]{2,1,0:T(8,128)(2,1)S(1)}, bf16[3,128,128]{2,1,0:T(8,128)(2,1)}, u32[]{:S(2)}) copy-start(bf16[3,128,128]{2,1,0:T(8,128)(2,1)} %refs_1_.2) | copy-start | bytes 294916
  0.6 24.9 %copy-start.1 = (s32[1,2]{1,0:T(1,128)S(1)}, s32[1,2]{1,0:T(1,128)}, u32[]{:S(2)}) copy-start(s32[1,2]{1,0:T(1,128)} %refs_2_.2) | copy-start | bytes 28

commit v9 on v7

--- a/solution.py
+++ b/solution.py
@@ -143,11 +143,11 @@
                         device_id_type=MESH,
                     ).start()
 
+        give_to(1, partner, x_send, x_sem)
+
         @pl.when(reaches)
         def _():
             give_to(2, diagonal, z_send, z_sem)
-
-        give_to(1, partner, x_send, x_sem)
 
     def hand_out(y_from, piece):
         index = 2 * y_from + x

time: 26.9 us -> 26.9 us (level)
  no operation moved by 1% of the time
where the time goes in v9:
time: 26.9 us; the launch traced here: 26.5 us
  Pallas kernels  25.8 us (96%)
  between operations  0.67 us (2%)
    pallas_call x1, Pallas kernels, local(): pl.pallas_call(lambda *refs: exchange_kernel(n_energy, n_space, rows, *re...  24.6 us
    pallas_call x1, Pallas kernels, local(): pl.pallas_call(lambda *refs: product_kernel(n_space, *refs), out_shape=(j...  1.22 us

profile of v9, /device:TPU:512, one launch (start us, length us, event | category | flops | bytes accessed | tf_op | source)
XLA Modules:
  0.0 26.5 jit_solution(15545496582349151044)
XLA Ops:
  0.6 0.0 copy-start
  0.6 0.0 copy-start.1
  0.6 24.6 %exchange.1.refs_0_ = bf16[3,4,2,64,128]{4,3,2,1,0:T(8,128)(2,1)S(1)} custom-call(bf16[4,2,64,128]{3,2,1,0:T(8,128)(2,1)} %bitcast.7, bf16[512,256]{1,0:T(8,128)(2,1)} %constant.4.clone.refs_1_, bf16[512,512]{1,0:T(8,128)(2,1)} %constant.5.clone.refs_2_), custom_call_target="tpu_custom_call" | custom-call | tf_op jit(solution)/shard_map/exchange/pallas_call | solution.py:320
  25.2 0.0 copy-done
  25.2 0.0 copy-done.1
  25.2 1.2 %products.1 = (bf16[2,2,2,128,128]{4,3,2,1,0:T(8,128)(2,1)}, bf16[4,128,128]{2,1,0:T(8,128)(2,1)}) custom-call(bf16[3,4,2,64,128]{4,3,2,1,0:T(8,128)(2,1)S(1)} %exchange.1.refs_0_, bf16[3,128,128]{2,1,0:T(8,128)(2,1)S(1)} %copy-done, s32[1,2]{1,0:T(1,128)S(1)} %copy-done.1), custom_call_target="tpu_custom_call" | custom-call | tf_op jit(solution)/shard_map/products/pallas_call | solution.py:338
Async XLA Ops:
  0.6 24.6 %copy-start = (bf16[3,128,128]{2,1,0:T(8,128)(2,1)S(1)}, bf16[3,128,128]{2,1,0:T(8,128)(2,1)}, u32[]{:S(2)}) copy-start(bf16[3,128,128]{2,1,0:T(8,128)(2,1)} %refs_1_.2) | copy-start | bytes 294916
  0.6 24.6 %copy-start.1 = (s32[1,2]{1,0:T(1,128)S(1)}, s32[1,2]{1,0:T(1,128)}, u32[]{:S(2)}) copy-start(s32[1,2]{1,0:T(1,128)} %refs_2_.2) | copy-start | bytes 28

commit v10 on v7

--- a/solution.py
+++ b/solution.py
@@ -189,8 +189,8 @@
             axis=1,
         )
         real_parts, imag_parts = [], []
-        step = half // 2
-        for c in range(2):
+        step = half // 4
+        for c in range(4):
             real = jnp.dot(fwd[c * step:(c + 1) * step], stacked, preferred_element_type=jnp.float32)
             imag = jnp.dot(fwd[half + c * step:half + (c + 1) * step], stacked, preferred_element_type=jnp.float32)
             less_re, less_im = real[:, :half], imag[:, :half]

time: 26.9 us -> 27.3 us (1.015)
  Pallas kernels: 25.8 us -> 26.2 us
    pallas_call x1, Pallas kernels: 24.6 us -> 25 us  [local(): pl.pallas_call(lambda *refs: exchange_kernel(n_energy, n_space, rows, *re...]
where the time goes in v10:
time: 27.3 us; the launch traced here: 26.9 us
  Pallas kernels  26.2 us (96%)
  between operations  0.67 us (2%)
    pallas_call x1, Pallas kernels, local(): pl.pallas_call(lambda *refs: exchange_kernel(n_energy, n_space, rows, *re...  25 us
    pallas_call x1, Pallas kernels, local(): pl.pallas_call(lambda *refs: product_kernel(n_space, *refs), out_shape=(j...  1.23 us

profile of v10, /device:TPU:512, one launch (start us, length us, event | category | flops | bytes accessed | tf_op | source)
XLA Modules:
  0.0 26.9 jit_solution(9104095363784845494)
XLA Ops:
  0.6 0.0 copy-start
  0.6 0.0 copy-start.1
  0.6 25.0 %exchange.1.refs_0_ = bf16[3,4,2,64,128]{4,3,2,1,0:T(8,128)(2,1)S(1)} custom-call(bf16[4,2,64,128]{3,2,1,0:T(8,128)(2,1)} %bitcast.7, bf16[512,256]{1,0:T(8,128)(2,1)} %constant.4.clone.refs_1_, bf16[512,512]{1,0:T(8,128)(2,1)} %constant.5.clone.refs_2_), custom_call_target="tpu_custom_call" | custom-call | tf_op jit(solution)/shard_map/exchange/pallas_call | solution.py:320
  25.6 0.0 copy-done
  25.6 0.0 copy-done.1
  25.7 1.2 %products.1 = (bf16[2,2,2,128,128]{4,3,2,1,0:T(8,128)(2,1)}, bf16[4,128,128]{2,1,0:T(8,128)(2,1)}) custom-call(bf16[3,4,2,64,128]{4,3,2,1,0:T(8,128)(2,1)S(1)} %exchange.1.refs_0_, bf16[3,128,128]{2,1,0:T(8,128)(2,1)S(1)} %copy-done, s32[1,2]{1,0:T(1,128)S(1)} %copy-done.1), custom_call_target="tpu_custom_call" | custom-call | tf_op jit(solution)/shard_map/products/pallas_call | solution.py:338
Async XLA Ops:
  0.6 25.0 %copy-start = (bf16[3,128,128]{2,1,0:T(8,128)(2,1)S(1)}, bf16[3,128,128]{2,1,0:T(8,128)(2,1)}, u32[]{:S(2)}) copy-start(bf16[3,128,128]{2,1,0:T(8,128)(2,1)} %refs_1_.2) | copy-start | bytes 294916
  0.6 25.0 %copy-start.1 = (s32[1,2]{1,0:T(1,128)S(1)}, s32[1,2]{1,0:T(1,128)}, u32[]{:S(2)}) copy-start(s32[1,2]{1,0:T(1,128)} %refs_2_.2) | copy-start | bytes 28
